TPU v7x, 256 devices: a whole 4x4x8 slice. The times are simulated.
256 devices in a mesh: gz: 8 (over x, core), xy: 32 (over y, z).
Axes of the slice: x: 4, y: 4, z: 8, core: 2. Of those that a mesh axis runs over, the one named last changes fastest.
Arguments:
- x_start: float32 [2, 8, 64, 512, 128], P(None, None, 'gz', 'xy'), may hold values from -6 to 6
- rhs: float32 [2, 8, 64, 512, 128], P(None, None, 'gz', 'xy'), may hold values from -20 to 20
- wave_sq: float32 [64, 512, 128], P('gz', 'xy'), may hold values from 0.3 to 1.5
- damping: float32 [64, 512, 128], P('gz', 'xy'), may hold values from 0.05 to 0.6
- front: float32 [2, 8192, 8192], P(None, ('gz', 'xy')), may hold values from -0.0703125 to 0.0703125
- front_order: int32 [8, 32, 32], P('gz', 'xy'), may hold values from 0 to 31, each once within a row
- pair_count: int32 [8, 32, 32], P('gz'), may hold values from 0 to 3, as said below
- sep_cell: int32 [8, 32, 96], P('gz', 'xy'), may hold values from 0 to 14463, as said below
Outputs:
- solution: float32 [2, 8, 64, 512, 128], P(None, None, 'gz', 'xy')
- new_residual: float32 [2, 8, 64, 512, 128], P(None, None, 'gz', 'xy')
Inputs may be any that keep to these rules, and one draw needn't show every extreme that they name: pair_count[g, o, t] counts the separator cells of brick (g, t) whose front rows belong to owner (g, o). For each g and o exactly one brick has 3, one has 2, 27 have 1 and all others 0, so they sum to 32; which bricks is drawn anew for each owner. `sep_cell`: the 96 entries of one brick are distinct local cell indices of that brick, each on its lowest z plane (z = 0) or its lowest y plane (y = 0). Each row front_order[g, o] is a permutation.
All inputs are finite; a program needn't handle non-finite values.
Results may differ from a plain program's by a relative error of at most 0.00011.
Values sent between devices are 32-bit elements; how exact they have to be, the bound alone decides.
A program may use at most 64 MiB of HBM per device.

v0:
```python
from functools import partial

import jax
import jax.numpy as jnp
from jax import lax
from jax.sharding import PartitionSpec as P


def extended(block, sides, width):
    for axis, dim in sides:
        count = lax.axis_size(axis)
        forward = [(i, i + 1) for i in range(count - 1)]
        backward = [(target, source) for source, target in forward]
        low = lax.ppermute(
            lax.slice_in_dim(block, block.shape[dim] - width, None, axis=dim), axis, forward
        )
        high = lax.ppermute(lax.slice_in_dim(block, 0, width, axis=dim), axis, backward)
        block = jnp.concatenate([low, block, high], axis=dim)
    return block


def apply_operator(padded, wave_sq, damping):
    depth, height, width = wave_sq.shape
    centre = padded[:, :, 1 : depth + 1, 1 : height + 1, 1 : width + 1]
    face_sum = jnp.zeros_like(centre)
    edge_sum = jnp.zeros_like(centre)
    corner_sum = jnp.zeros_like(centre)
    for offset_z in (-1, 0, 1):
        for offset_y in (-1, 0, 1):
            for offset_x in (-1, 0, 1):
                nonzero = abs(offset_z) + abs(offset_y) + abs(offset_x)
                if nonzero == 0:
                    continue
                shifted = padded[
                    :,
                    :,
                    1 + offset_z : 1 + offset_z + depth,
                    1 + offset_y : 1 + offset_y + height,
                    1 + offset_x : 1 + offset_x + width,
                ]
                if nonzero == 1:
                    face_sum = face_sum + shifted
                elif nonzero == 2:
                    edge_sum = edge_sum + shifted
                else:
                    corner_sum = corner_sum + shifted
    negative_laplace = (128.0 * centre - 14.0 * face_sum - 3.0 * edge_sum - corner_sum) / 30.0
    real_part = negative_laplace[0] - wave_sq * (centre[0] - damping * centre[1])
    imag_part = negative_laplace[1] - wave_sq * (centre[1] + damping * centre[0])
    return jnp.stack([real_part, imag_part])


def scale_diagonal(field, wave_sq, damping):
    diag_real = 128.0 / 30.0 - wave_sq
    diag_imag = -wave_sq * damping
    modulus = diag_real * diag_real + diag_imag * diag_imag
    return jnp.stack(
        [
            (field[0] * diag_real + field[1] * diag_imag) / modulus,
            (field[1] * diag_real - field[0] * diag_imag) / modulus,
        ]
    )


def pad_width(field):
    return jnp.pad(field, ((0, 0), (0, 0), (0, 0), (0, 0), (1, 1)))


def extend(field):
    padded = extended(field, (("gz", 2), ("xy", 3)), 1)
    return pad_width(padded)


def local(x_start, rhs, wave_sq, damping, front, front_order, pair_count, sep_cell):
    highest = lax.Precision.HIGHEST
    rhs_count = x_start.shape[1]
    components = 2 * rhs_count
    tiles = pair_count.shape[1]
    rows_own = front_order.shape[2]
    slots = sep_cell.shape[2]
    capacity = slots // tiles
    cell_total = wave_sq.size
    own_index = lax.axis_index("xy")
    residual = rhs - apply_operator(extend(x_start), wave_sq, damping)
    scaled = scale_diagonal(residual, wave_sq, damping)
    counts = pair_count[0]
    offsets = jnp.cumsum(counts, axis=1) - counts
    sep_cells = sep_cell[0, 0]
    slot_ids = jnp.arange(slots, dtype=jnp.int32)
    rank_in = slot_ids % capacity
    owner_of = slot_ids // capacity
    sent_counts = lax.dynamic_index_in_dim(counts, own_index, 1, keepdims=False)
    sent_offsets = lax.dynamic_index_in_dim(offsets, own_index, 1, keepdims=False)
    valid_send = (rank_in < sent_counts[owner_of]).astype(jnp.float32)
    flat_residual = residual.reshape(components, cell_total)
    slot_vals = jnp.take(flat_residual, sep_cells, axis=1) * valid_send[None, :]
    got_counts = lax.dynamic_index_in_dim(counts, own_index, 0, keepdims=False)
    got_offsets = lax.dynamic_index_in_dim(offsets, own_index, 0, keepdims=False)
    entry = got_offsets[owner_of] + rank_in
    valid_got = rank_in < got_counts[owner_of]
    row_ids = jnp.arange(rows_own, dtype=jnp.int32)
    entry_map = (valid_got[:, None] & (entry[:, None] == row_ids[None, :])).astype(jnp.float32)
    order_map = (front_order[0, 0][:, None] == row_ids[None, :]).astype(jnp.float32)
    all_slots = lax.all_gather(slot_vals, "xy", axis=1, tiled=True)
    received = lax.dynamic_index_in_dim(
        all_slots.reshape(components, tiles, tiles, capacity), own_index, 2, keepdims=False
    ).reshape(components, slots)
    by_entry = jnp.dot(received, entry_map, precision=highest, preferred_element_type=jnp.float32)
    owned = jnp.dot(by_entry, order_map, precision=highest, preferred_element_type=jnp.float32)
    front_real = front[0]
    front_imag = front[1]
    product = partial(
        lax.dot_general,
        dimension_numbers=(((1,), (1,)), ((), ())),
        precision=highest,
        preferred_element_type=jnp.float32,
    )
    blank = jnp.zeros((rows_own, rhs_count), jnp.float32)
    part_vals = lax.all_gather(owned, ("gz", "xy"), axis=1, tiled=True)
    vals_real = part_vals[:rhs_count]
    vals_imag = part_vals[rhs_count:]
    new_real = blank + product(front_real, vals_real) - product(front_imag, vals_imag)
    new_imag = blank + product(front_real, vals_imag) + product(front_imag, vals_real)
    solved = jnp.concatenate([new_real.T, new_imag.T], axis=0)
    solved_entry = jnp.dot(
        solved, order_map.T, precision=highest, preferred_element_type=jnp.float32
    )
    owner_rows = lax.all_gather(solved_entry, "xy", axis=1, tiled=True)
    pick = jnp.minimum(owner_of * rows_own + sent_offsets[owner_of] + rank_in, tiles * rows_own - 1)
    returned = jnp.take(owner_rows, pick, axis=1) * valid_send[None, :]
    correction = (
        jnp.zeros((components, cell_total), jnp.float32)
        .at[:, sep_cells]
        .add(returned)
        .reshape(residual.shape)
    )
    direction = scaled + correction
    image = apply_operator(extend(direction), wave_sq, damping)
    num_real = jnp.sum(image[0] * residual[0] + image[1] * residual[1], axis=(1, 2, 3))
    num_imag = jnp.sum(image[0] * residual[1] - image[1] * residual[0], axis=(1, 2, 3))
    den_part = jnp.sum(image[0] * image[0] + image[1] * image[1], axis=(1, 2, 3))
    totals = lax.psum(jnp.stack([num_real, num_imag, den_part]), ("gz", "xy"))
    denom = totals[2] + 1e-06
    alpha_real = (totals[0] / denom)[:, None, None, None]
    alpha_imag = (totals[1] / denom)[:, None, None, None]
    solution = jnp.stack(
        [
            x_start[0] + alpha_real * direction[0] - alpha_imag * direction[1],
            x_start[1] + alpha_real * direction[1] + alpha_imag * direction[0],
        ]
    )
    new_residual = jnp.stack(
        [
            residual[0] - alpha_real * image[0] + alpha_imag * image[1],
            residual[1] - alpha_real * image[1] - alpha_imag * image[0],
        ]
    )
    return (solution, new_residual)


def solution(mesh):
    in_specs = (
        P(None, None, "gz", "xy", None),
        P(None, None, "gz", "xy", None),
        P("gz", "xy", None),
        P("gz", "xy", None),
        P(None, ("gz", "xy"), None),
        P("gz", "xy", None),
        P("gz", None, None),
        P("gz", "xy", None),
    )
    out_specs = (P(None, None, "gz", "xy", None), P(None, None, "gz", "xy", None))
    return jax.shard_map(local, mesh=mesh, in_specs=in_specs, out_specs=out_specs, check_vma=False)
```

profile of v0, /device:TPU:1, one launch (start us, length us, event | category | flops | bytes accessed | tf_op | source)
XLA Modules:
  0.0 355.8 jit_solution(13634245641871823886)
XLA Ops:
  0.7 1.1 fusion.91
  1.8 4.5 %collective-permute-start = (f32[2,8,1,16,128]{4,3,2,1,0:T(8,128)S(1)}, f32[2,8,1,16,128]{4,3,2,1,0:T(8,128)S(1)}, u32[]{:S(2)}, u32[]{:S(2)}) collective-permute-start(f32[2,8,1,16,128]{4,3,2,1,0:T(8,128)S(1)} %get-tuple-element.29), channel_id=1, source_target_pairs={{0,32},{32,64},{64,96},{96,128},{128,160},{160,192},{192,224},{1,3... | collective-permute-start | bytes 393224 | tf_op jit(solution)/shard_map/ppermute | solution.py:14
  6.3 1.9 collective-permute-start.1
  8.2 0.9 dynamic-slice_reduce_fusion
  9.1 0.7 fusion.78
  9.8 0.9 reduce_window_sum.11
  10.7 0.7 bitcast_subtract_fusion.1
  11.4 0.2 dynamic-slice_reduce_fusion.1
  11.6 1.2 gather_fusion
  12.9 0.7 fusion.80
  13.6 1.2 gather_fusion.2
  14.8 0.7 compare_convert_fusion
  15.5 1.2 gather_fusion.4
  16.7 1.2 gather_fusion.3
  18.0 0.7 multiply_add_fusion.2
  19.0 3.5 collective-permute-start.2
  22.6 1.3 collective-permute-start.3
  24.0 3.9 %collective-permute-done.3 = f32[2,8,10,1,128]{4,3,2,1,0:T(1,128)S(1)} collective-permute-done((f32[2,8,10,1,128]{4,3,2,1,0:T(1,128)S(1)}, f32[2,8,10,1,128]{4,3,2,1,0:T(1,128)S(1)}, u32[]{:S(2)}, u32[]{:S(2)}) %collective-permute-start.3) | collective-permute-done | bytes 81952 | tf_op jit(solution)/shard_map/ppermute | solution.py:17
  27.9 0.6 copy-done.6
  28.6 1.8 select_maximum_fusion.4
  30.3 5.6 %fusion.16 = f32[2,8,8,16,128]{4,3,2,1,0:T(8,128)} fusion(f32[2,8,10,16,128]{4,3,2,1,0:T(8,128)S(1)} %constant_dynamic-update-slice_fusion, f32[2,8,10,1,128]{4,3,2,1,0:T(1,128)} %copy-done.6, f32[2,8,10,1,128]{4,3,2,1,0:T(1,128)} %copy-done.5, f32[2,8,10,18,130]{4,3,2,1,0:T(8,128)S(1)} %select_maximum_fusion.4, ...), kind=kLoop, calls=%fused_computation.45 | loop fusion | flops 9961472 | bytes 22708224 | tf_op jit(solution)/shard_map/div | solution.py:47
  35.9 1.5 slice_subtract_fusion.1
  37.6 0.2 reshape.193
  37.8 4.6 %copy.23 = f32[16,16384]{0,1:T(8,128)} copy(f32[16,16384]{1,0:T(8,128)S(1)} %reshape.193) | data formatting | bytes 2097152 | tf_op jit(solution)/shard_map/reshape | solution.py:95
  42.4 4.0 %gather_fusion.1 = f32[96,16]{1,0:T(8,128)S(1)} fusion(f32[16,16384]{0,1:T(8,128)} %copy.23, s32[1024]{0:T(1024)S(1)} %pad_clamp_fusion.1), kind=kCustom, calls=%fused_computation.1 | custom fusion | bytes 12672 | tf_op jit(solution)/shard_map/jit(_take)/gather | solution.py:96
  46.6 40.5 %all-gather = f32[32,96,16]{1,2,0:T(8,128)S(1)} all-gather(f32[1,96,16]{1,2,0:T(8,128)S(1)} %copy.24), channel_id=1, replica_groups=mesh['gz'=8,'xy'=32] {'xy'}, dimensions={0}, use_global_device_ids=true | all-gather | bytes 202752 | tf_op jit(solution)/shard_map/all_gather | solution.py:104
  87.2 0.2 reshape.254
  87.4 0.5 copy.26
  87.8 1.7 reshape.194
  89.6 0.9 constant_dynamic-slice_fusion.2
  90.5 0.2 fusion.61
  90.7 0.2 convolution_bitcast_fusion.1
  90.9 81.8 %all-gather.1 = f32[256,32,16]{1,2,0:T(8,128)S(1)} all-gather(f32[1,32,16]{1,2,0:T(8,128)S(1)} %convolution_bitcast_fusion.1), channel_id=1, replica_groups=mesh['gz'=8,'xy'=32] {'gz','xy'}, dimensions={0}, use_global_device_ids=true | all-gather | bytes 526336 | tf_op jit(solution)/shard_map/all_gather | solution.py:119
  172.7 2.0 copy.27
  174.7 2.5 reshape.256
  177.3 2.3 fusion.40
  179.6 2.2 fusion.38
  181.7 0.9 convolution_subtract_fusion
  182.7 1.0 convolution_add_fusion
  183.6 0.2 convolution_bitcast_fusion
  183.8 36.2 %all-gather.2 = f32[32,32,16]{1,2,0:T(8,128)S(1)} all-gather(f32[1,32,16]{1,2,0:T(8,128)S(1)} %convolution_bitcast_fusion), channel_id=1, replica_groups=mesh['gz'=8,'xy'=32] {'xy'}, dimensions={0}, use_global_device_ids=true | all-gather | bytes 67584 | tf_op jit(solution)/shard_map/all_gather | solution.py:128
  220.0 0.2 copy.31
  220.2 5.0 %scatter_custom_fusion = f32[16,16384]{0,1:T(8,128)} fusion(s32[96]{0:T(128)S(1)} %fusion.80, f32[]{:T(128)} %constant.81.clone.1, f32[96]{0:T(128)S(1)} %get-tuple-element.33, f32[]{:T(128)} %constant.96.clone.1, pred[96]{0:T(512)(128)(4,1)S(1)} %compare_and_fusion.1, f32[16,1024]{0,1:T(8,128)S(1)} %bitcast.110, s32[1024]{0:T(1024)S(1)} %pad_clamp_fusion), kind=kCustom, calls=%fused_computation.9 | custom fusion | flops 4608 | bytes 1577992 | tf_op jit(solution)/shard_map/scatter-add | solution.py:134
  225.2 5.1 %copy.30 = f32[16,16384]{1,0:T(8,128)S(1)} copy(f32[16,16384]{0,1:T(8,128)} %scatter_custom_fusion) | data formatting | bytes 2097152 | tf_op jit(solution)/shard_map/scatter-add | solution.py:134
  230.3 0.2 copy.33
  230.6 0.6 copy-done.7
  231.2 0.2 add_divide_fusion
  231.4 0.2 maximum_add_fusion
  231.6 15.0 %collective-permute-start.4 = (f32[2,8,1,16,128]{4,3,2,1,0:T(8,128)S(1)}, f32[2,8,1,16,128]{4,3,2,1,0:T(8,128)S(1)}, u32[]{:S(2)}, u32[]{:S(2)}) collective-permute-start(f32[2,8,1,16,128]{4,3,2,1,0:T(8,128)S(1)} %get-tuple-element.26), channel_id=1, source_target_pairs={{0,32},{32,64},{64,96},{96,128},{128,160},{160,192},{192,224},{1,3... | collective-permute-start | bytes 393224 | tf_op jit(solution)/shard_map/ppermute | solution.py:14
  246.6 3.0 collective-permute-start.5
  249.6 3.3 collective-permute-done.5
  253.0 3.0 collective-permute-start.6
  256.0 1.5 collective-permute-start.7
  257.5 3.7 %collective-permute-done.7 = f32[2,8,10,1,128]{4,3,2,1,0:T(1,128)S(1)} collective-permute-done((f32[2,8,10,1,128]{4,3,2,1,0:T(1,128)S(1)}, f32[2,8,10,1,128]{4,3,2,1,0:T(1,128)S(1)}, u32[]{:S(2)}, u32[]{:S(2)}) %collective-permute-start.7) | collective-permute-done | bytes 81952 | tf_op jit(solution)/shard_map/ppermute | solution.py:17
  261.2 2.3 maximum_maximum_fusion
  263.5 2.7 select_maximum_fusion
  266.2 6.5 %fusion.30 = f32[2,8,8,16,128]{4,3,2,1,0:T(8,128)} fusion(f32[2,8,10,18,130]{4,3,2,1,0:T(8,128)S(1)} %select_maximum_fusion, f32[2,8,10,17,128]{4,3,2,1,0:T(8,128)} %get-tuple-element.17, f32[2,8,10,17,128]{4,3,2,1,0:T(8,128)} %get-tuple-element.16, f32[2,8,1,16,128]{4,3,2,1,0:T(8,128)S(1)} %collective-permute-done.5, ...), kind=kLoop, calls=%fused_computation.60 | loop fusion | flops 8388608 | bytes 27525120 | tf_op jit(solution)/shard_map/div | solution.py:47
  272.7 1.4 fusion.52
  274.1 0.4 fusion.47
  274.4 77.1 %psum.7 = f32[3,8]{1,0:T(4,128)S(1)} all-reduce(f32[3,8]{1,0:T(4,128)S(1)} %pad_maximum_fusion.12), channel_id=1, replica_groups=mesh['gz'=8,'xy'=32] {'gz','xy'}, use_global_device_ids=true, to_apply=%region_5.6 | all-reduce | flops 24 | bytes 192 | tf_op jit(solution)/shard_map/psum | solution.py:142
  351.5 2.0 multiply_add_fusion
  353.5 0.2 multiply_subtract_fusion
  353.7 1.0 pad_maximum_fusion.8
  354.8 1.0 pad_maximum_fusion.7
  (47 shorter events, 1.2 us)
Async XLA Ops:
  0.6 18.1 %copy-start = (f32[2,8,8,16,128]{4,3,2,1,0:T(8,128)S(1)}, f32[2,8,8,16,128]{4,3,2,1,0:T(8,128)}, u32[]{:S(2)}) copy-start(f32[2,8,8,16,128]{4,3,2,1,0:T(8,128)} %param.8) | copy-start | bytes 3145732
  0.6 17.3 %copy-start.3 = (f32[8,16,128]{2,1,0:T(8,128)S(1)}, f32[8,16,128]{2,1,0:T(8,128)}, u32[]{:S(2)}) copy-start(f32[8,16,128]{2,1,0:T(8,128)} %param.10) | copy-start | bytes 196612
  0.7 17.3 %copy-start.2 = (f32[8,16,128]{2,1,0:T(8,128)S(1)}, f32[8,16,128]{2,1,0:T(8,128)}, u32[]{:S(2)}) copy-start(f32[8,16,128]{2,1,0:T(8,128)} %param.11) | copy-start | bytes 196612
  1.8 17.0 %collective-permute-start = (f32[2,8,1,16,128]{4,3,2,1,0:T(8,128)S(1)}, f32[2,8,1,16,128]{4,3,2,1,0:T(8,128)S(1)}, u32[]{:S(2)}, u32[]{:S(2)}) collective-permute-start(f32[2,8,1,16,128]{4,3,2,1,0:T(8,128)S(1)} %get-tuple-element.29), channel_id=1, source_target_pairs={{0,32},{32,64},{64,96},{96,128},{128,160},{160,192},{192,224},{1,3... | collective-permute-start | bytes 393224 | tf_op jit(solution)/shard_map/ppermute | solution.py:14
  6.3 12.6 %collective-permute-start.1 = (f32[2,8,1,16,128]{4,3,2,1,0:T(8,128)S(1)}, f32[2,8,1,16,128]{4,3,2,1,0:T(8,128)S(1)}, u32[]{:S(2)}, u32[]{:S(2)}) collective-permute-start(f32[2,8,1,16,128]{4,3,2,1,0:T(8,128)S(1)} %get-tuple-element.28), channel_id=1, source_target_pairs={{32,0},{64,32},{96,64},{128,96},{160,128},{192,160},{224,192},{33,... | collective-permute-start | bytes 393224 | tf_op jit(solution)/shard_map/ppermute | solution.py:17
  19.0 5.0 %collective-permute-start.2 = (f32[2,8,10,1,128]{4,3,2,1,0:T(1,128)S(1)}, f32[2,8,10,1,128]{4,3,2,1,0:T(1,128)S(1)}, u32[]{:S(2)}, u32[]{:S(2)}) collective-permute-start(f32[2,8,10,1,128]{4,3,2,1,0:T(1,128)S(1)} %get-tuple-element.20), channel_id=1, source_target_pairs={{0,1},{1,2},{2,3},{3,4},{4,5},{5,6},{6,7},{7,8},{8,9},{9,10},{10,1... | collective-permute-start | bytes 245768 | tf_op jit(solution)/shard_map/ppermute | solution.py:14
  22.6 5.4 %collective-permute-start.3 = (f32[2,8,10,1,128]{4,3,2,1,0:T(1,128)S(1)}, f32[2,8,10,1,128]{4,3,2,1,0:T(1,128)S(1)}, u32[]{:S(2)}, u32[]{:S(2)}) collective-permute-start(f32[2,8,10,1,128]{4,3,2,1,0:T(1,128)S(1)} %get-tuple-element.21), channel_id=1, source_target_pairs={{1,0},{2,1},{3,2},{4,3},{5,4},{6,5},{7,6},{8,7},{9,8},{10,9},{11,1... | collective-permute-start | bytes 245768 | tf_op jit(solution)/shard_map/ppermute | solution.py:17
  24.0 3.9 %copy-start.5 = (f32[2,8,10,1,128]{4,3,2,1,0:T(1,128)}, f32[2,8,10,1,128]{4,3,2,1,0:T(1,128)S(1)}, u32[]{:S(2)}) copy-start(f32[2,8,10,1,128]{4,3,2,1,0:T(1,128)S(1)} %collective-permute-done.2) | copy-start | bytes 245764
  27.9 0.6 copy-start.6
  35.9 1.5 copy-start.4
  87.8 2.9 copy-start.10
  177.3 4.5 %copy-start.1 = (f32[2,32,8192]{2,1,0:T(8,128)S(1)}, f32[2,32,8192]{2,1,0:T(8,128)}, u32[]{:S(2)}) copy-start(f32[2,32,8192]{2,1,0:T(8,128)} %param.12) | copy-start | bytes 6291460
  230.3 0.9 copy-start.7
  230.3 0.9 copy-start.8
  230.3 0.9 copy-start.9
  231.6 18.0 %collective-permute-start.4 = (f32[2,8,1,16,128]{4,3,2,1,0:T(8,128)S(1)}, f32[2,8,1,16,128]{4,3,2,1,0:T(8,128)S(1)}, u32[]{:S(2)}, u32[]{:S(2)}) collective-permute-start(f32[2,8,1,16,128]{4,3,2,1,0:T(8,128)S(1)} %get-tuple-element.26), channel_id=1, source_target_pairs={{0,32},{32,64},{64,96},{96,128},{128,160},{160,192},{192,224},{1,3... | collective-permute-start | bytes 393224 | tf_op jit(solution)/shard_map/ppermute | solution.py:14
  246.6 6.3 %collective-permute-start.5 = (f32[2,8,1,16,128]{4,3,2,1,0:T(8,128)S(1)}, f32[2,8,1,16,128]{4,3,2,1,0:T(8,128)S(1)}, u32[]{:S(2)}, u32[]{:S(2)}) collective-permute-start(f32[2,8,1,16,128]{4,3,2,1,0:T(8,128)S(1)} %get-tuple-element.27), channel_id=1, source_target_pairs={{32,0},{64,32},{96,64},{128,96},{160,128},{192,160},{224,192},{33,... | collective-permute-start | bytes 393224 | tf_op jit(solution)/shard_map/ppermute | solution.py:17
  253.0 4.5 %collective-permute-start.6 = (f32[2,8,10,1,128]{4,3,2,1,0:T(1,128)S(1)}, f32[2,8,10,1,128]{4,3,2,1,0:T(1,128)S(1)}, u32[]{:S(2)}, u32[]{:S(2)}) collective-permute-start(f32[2,8,10,1,128]{4,3,2,1,0:T(1,128)S(1)} %get-tuple-element.18), channel_id=1, source_target_pairs={{0,1},{1,2},{2,3},{3,4},{4,5},{5,6},{6,7},{7,8},{8,9},{9,10},{10,1... | collective-permute-start | bytes 245768 | tf_op jit(solution)/shard_map/ppermute | solution.py:14
  256.0 5.2 %collective-permute-start.7 = (f32[2,8,10,1,128]{4,3,2,1,0:T(1,128)S(1)}, f32[2,8,10,1,128]{4,3,2,1,0:T(1,128)S(1)}, u32[]{:S(2)}, u32[]{:S(2)}) collective-permute-start(f32[2,8,10,1,128]{4,3,2,1,0:T(1,128)S(1)} %get-tuple-element.19), channel_id=1, source_target_pairs={{1,0},{2,1},{3,2},{4,3},{5,4},{6,5},{7,6},{8,7},{9,8},{10,9},{11,1... | collective-permute-start | bytes 245768 | tf_op jit(solution)/shard_map/ppermute | solution.py:17
where the time goes:
time: 357 us; the launch traced here: 356 us
  blocking collectives  236 us (66%)
  other arithmetic  35.8 us (10%)
  starting transfers between devices  33.7 us (9%)
  local copies, waits for them, and re-layouts  31.7 us (9%)
  waiting for transfers between devices  11 us (3%)
  matrix products  6.99 us (2%)
    all_gather x1, blocking collectives, local(): part_vals = lax.all_gather(owned, ('gz', 'xy'), axis=1, tiled=True)  81.8 us
    psum x1, blocking collectives, local(): totals = lax.psum(jnp.stack([num_real, num_imag, den_part]), ('gz', 'xy'))  77.1 us
    all_gather x1, blocking collectives, local(): all_slots = lax.all_gather(slot_vals, 'xy', axis=1, tiled=True)  40.5 us
    all_gather x1, blocking collectives, local(): owner_rows = lax.all_gather(solved_entry, 'xy', axis=1, tiled=True)  36.2 us
    ppermute x4, starting transfers between devices, extended(): lax.ppermute(lax.slice_in_dim(block, block.shape[dim] - width, None, axis...  26 us
    div x2, other arithmetic, apply_operator(): (128.0 * centre - 14.0 * face_sum - 3.0 * edge_sum - corner_sum) / 30.0  12 us
    ppermute x4, waiting for transfers between devices, extended(): lax.ppermute(lax.slice_in_dim(block, 0, width, axis=dim), axis, backward)  10.9 us
    ppermute x4, starting transfers between devices, extended(): lax.ppermute(lax.slice_in_dim(block, 0, width, axis=dim), axis, backward)  7.72 us
  transfers between devices with their start and end apart: 8, of which 4 were waited for; matrix products, arithmetic and copies ran while one was open for 3% of the time, Pallas kernels for 0%

commit v1 on v0

v1 whole, which is shorter than its diff:
```python
import functools

import jax
import jax.numpy as jnp
from jax import lax
from jax.experimental import pallas as pl
from jax.experimental.pallas import tpu as pltpu
from jax.sharding import PartitionSpec as P

MESH = pl.DeviceIdType.MESH
HIGHEST = lax.Precision.HIGHEST
F32 = jnp.float32
BF16 = jnp.bfloat16
LANES = 128


def iota(shape, dim):
    return lax.broadcasted_iota(jnp.int32, shape, dim)


def dot(a, b, contract):
    return lax.dot_general(
        a, b, ((contract[:1], contract[1:]), ((), ())), precision=HIGHEST, preferred_element_type=F32
    )


def x_sum(u):
    axis = u.ndim - 1
    lane = iota(u.shape, axis)
    left = jnp.where(lane > 0, pltpu.roll(u, 1, axis), 0.0)
    right = jnp.where(lane < LANES - 1, pltpu.roll(u, LANES - 1, axis), 0.0)
    return left + right


def side_rows(rows, edge_low, edge_high):
    depth = rows.shape[0]
    row_sum = x_sum(rows)
    m1 = 14.0 * rows + 3.0 * row_sum
    m2 = 3.0 * rows + row_sum
    edge = jnp.where(iota(rows.shape, 0) == 0, edge_low, edge_high)
    m2_edge = 3.0 * edge + x_sum(edge)
    z_pos = iota(rows.shape, 0)
    below = jnp.where(z_pos == 0, m2_edge, pltpu.roll(m2, 1, 0))
    above = jnp.where(z_pos == depth - 1, m2_edge, pltpu.roll(m2, depth - 1, 0))
    return m1 + below + above


def laplace(centre, z_low, z_high, y_low, y_high, edges):
    depth, height, _ = centre.shape
    padded = jnp.concatenate([z_low[None], centre, z_high[None]], axis=0)
    p = x_sum(padded)
    m1 = 14.0 * padded + 3.0 * p
    m2 = 3.0 * padded + p
    same = 128.0 * centre - 14.0 * p[1:-1] - (m1[:-2] + m1[2:])
    side = m1[1:-1] + m2[:-2] + m2[2:]
    low = side_rows(y_low, edges[0], edges[2])
    high = side_rows(y_high, edges[1], edges[3])
    y_pos = iota(centre.shape, 1)
    before = jnp.where(y_pos == 0, low[:, None, :], pltpu.roll(side, 1, 1))
    after = jnp.where(y_pos == height - 1, high[:, None, :], pltpu.roll(side, height - 1, 1))
    return (same - before - after) * (1.0 / 30.0)


def pack_slots(rows, tiles):
    lane = iota((tiles, LANES), 1)
    out = rows[:tiles]
    for k in range(1, 3):
        out = jnp.where(lane < 16 * k, out, pltpu.roll(rows[k * tiles : (k + 1) * tiles], 16 * k, 1))
    return out


def unpack_slots(rows):
    return jnp.concatenate([rows] + [pltpu.roll(rows, LANES - 16 * k, 1) for k in range(1, 3)], axis=0)


def step(
    x_hbm, rhs_hbm, wave_hbm, damp_hbm, front_hbm, order_ref, count_ref, cell_ref,
    sol_ref, new_ref,
    x, rhs, wave, damp, front, split, res, drn, img, coef,
    y_send, e_send, z_got, y_got, e_got,
    slot_send, slot_got, own_send, own_got, vectors, ret_send, ret_got, acc, sum_send, sum_got, sum2_send, sum2_got, alpha,
    load_sem, halo_send_sem, halo_recv_sem, tile_send_sem, tile_recv_sem, slab_send_sem, slab_recv_sem,
):
    slabs, tiles = lax.axis_size("gz"), lax.axis_size("xy")
    g, t = lax.axis_index("gz"), lax.axis_index("xy")
    rhs_count, depth, height = x.shape[1], x.shape[2], x.shape[3]
    comps = 2 * rhs_count
    up_g, down_g = lax.rem(g + 1, slabs), lax.rem(g + slabs - 1, slabs)
    up_t, down_t = lax.rem(t + 1, tiles), lax.rem(t + tiles - 1, tiles)

    loads = [
        pltpu.make_async_copy(src, dst, load_sem.at[i])
        for i, (src, dst) in enumerate(
            [(x_hbm, x), (rhs_hbm, rhs), (wave_hbm, wave), (damp_hbm, damp), (front_hbm, front)]
        )
    ]
    for copy in loads:
        copy.start()

    barrier = pltpu.get_barrier_semaphore()

    def greet(gz, xy):
        pl.semaphore_signal(barrier, inc=1, device_id={"gz": gz, "xy": xy}, device_id_type=MESH)

    def greet_tile(j, carry):
        greet(g, lax.rem(t + j, tiles))
        return carry

    def greet_slab(j, carry):
        greet(lax.rem(g + j, slabs), t)
        return carry

    lax.fori_loop(1, tiles, greet_tile, 0)
    lax.fori_loop(1, slabs, greet_slab, 0)
    for gz in (up_g, down_g):
        for xy in (up_t, down_t):
            greet(gz, xy)

    def remote(src, dst, send_sem, recv_sem, gz, xy):
        return pltpu.make_async_remote_copy(
            src_ref=src, dst_ref=dst, send_sem=send_sem, recv_sem=recv_sem,
            device_id={"gz": gz, "xy": xy}, device_id_type=MESH,
        )

    def pack_halo(field, which):
        low, high = field[:, :, :, 0, :], field[:, :, :, height - 1, :]
        y_send[which, 0] = low
        y_send[which, 1] = high
        e_send[which, 0] = high[:, :, depth - 1, :]
        e_send[which, 1] = low[:, :, depth - 1, :]
        e_send[which, 2] = high[:, :, 0, :]
        e_send[which, 3] = low[:, :, 0, :]

    def halo_copies(field, which):
        todo = [
            (field.at[:, :, depth - 1], z_got.at[which, 0], up_g, t),
            (field.at[:, :, 0], z_got.at[which, 1], down_g, t),
            (y_send.at[which, 1], y_got.at[which, 0], g, up_t),
            (y_send.at[which, 0], y_got.at[which, 1], g, down_t),
            (e_send.at[which, 0], e_got.at[which, 0], up_g, up_t),
            (e_send.at[which, 1], e_got.at[which, 1], up_g, down_t),
            (e_send.at[which, 2], e_got.at[which, 2], down_g, up_t),
            (e_send.at[which, 3], e_got.at[which, 3], down_g, down_t),
        ]
        return [
            remote(src, dst, halo_send_sem.at[which, i], halo_recv_sem.at[which, i], gz, xy)
            for i, (src, dst, gz, xy) in enumerate(todo)
        ]

    has_down_g = (g > 0).astype(F32)
    has_up_g = (g < slabs - 1).astype(F32)
    has_down_t = (t > 0).astype(F32)
    has_up_t = (t < tiles - 1).astype(F32)

    def operator(field, which, r):
        parts = []
        for k in range(2):
            edges = [
                e_got[which, i, k, pl.ds(r, 1), :] * flag
                for i, flag in enumerate(
                    [has_down_g * has_down_t, has_down_g * has_up_t, has_up_g * has_down_t, has_up_g * has_up_t]
                )
            ]
            parts.append(
                laplace(
                    field[k, r],
                    z_got[which, 0, k, r] * has_down_g,
                    z_got[which, 1, k, r] * has_up_g,
                    y_got[which, 0, k, r] * has_down_t,
                    y_got[which, 1, k, r] * has_up_t,
                    edges,
                )
            )
        re, im = field[0, r], field[1, r]
        w, wd = wave[...], damp[...]
        return parts[0] - w * re + wd * im, parts[1] - w * im - wd * re

    def send_rows(send, got, bank):
        def start(j, carry):
            peer = lax.rem(t + j, tiles)
            remote(
                send.at[peer], got.at[t], tile_send_sem.at[bank, peer], tile_recv_sem.at[bank, t], g, peer
            ).start()
            return carry

        lax.fori_loop(1, tiles, start, 0)

    def wait_rows(send, got, bank):
        def wait(j, carry):
            peer = lax.rem(t + j, tiles)
            remote(
                send.at[peer], got.at[peer], tile_send_sem.at[bank, peer], tile_recv_sem.at[bank, peer], g, peer
            ).wait()
            return carry

        lax.fori_loop(1, tiles, wait, 0)

    def spread(send, got, bank):
        def start(j, carry):
            peer = lax.rem(t + j, tiles)
            remote(send, got.at[t], tile_send_sem.at[bank, peer], tile_recv_sem.at[bank, t], g, peer).start()
            return carry

        lax.fori_loop(1, tiles, start, 0)

    def wait_spread(send, got, bank):
        def wait(j, carry):
            peer = lax.rem(t + j, tiles)
            remote(
                send, got.at[peer], tile_send_sem.at[bank, peer], tile_recv_sem.at[bank, peer], g, peer
            ).wait()
            return carry

        lax.fori_loop(1, tiles, wait, 0)

    loads[0].wait()
    pack_halo(x, 0)
    x_halo = halo_copies(x, 0)
    pl.semaphore_wait(barrier, tiles - 1 + slabs - 1 + 4)
    for copy in x_halo:
        copy.start()

    loads[2].wait()
    loads[3].wait()
    w = wave[...]
    wd = w * damp[...]
    damp[...] = wd
    diag_re = 128.0 / 30.0 - w
    diag_im = -wd
    modulus = diag_re * diag_re + diag_im * diag_im
    coef[0] = diag_re / modulus
    coef[1] = diag_im / modulus

    counts = count_ref[0, pl.ds(t, 1), :].astype(F32)
    spread_lane = iota((tiles, LANES), 1)
    spread_row = iota((tiles, LANES), 0)
    rank = spread_lane // tiles
    live = spread_lane < 3 * tiles
    take = jnp.where(live & (spread_row == spread_lane % tiles), 1.0, 0.0)
    earlier = jnp.where(live & (spread_row < spread_lane % tiles), 1.0, 0.0)
    counts8 = jnp.broadcast_to(counts, (8, tiles))
    count_at = dot(counts8, take, (1, 0))[:1]
    entry_at = dot(counts8, earlier, (1, 0))[:1] + rank[:1].astype(F32)
    entry_map = jnp.where((rank.astype(F32) < count_at) & (spread_row.astype(F32) == entry_at), 1.0, 0.0)
    order = order_ref[0, 0:1, :]
    order_map = jnp.where(iota((tiles, tiles), 0) == order, 1.0, 0.0)
    row_map = dot(order_map, entry_map, (1, 0))

    cells = jnp.broadcast_to(cell_ref[0, 0:1, :].astype(F32), (8, cell_ref.shape[2]))
    slots = cell_ref.shape[2]
    slot_row = iota((slots, LANES), 0)
    slot_lane = iota((slots, LANES), 1)
    slot_pick = jnp.where(
        (slot_lane < slots) & (slot_row == 3 * (slot_lane % tiles) + slot_lane // tiles), 1.0, 0.0
    )
    cell_at = (dot(cells, slot_pick, (1, 0))[:1] + 0.5).astype(jnp.int32)
    cell_x = cell_at % LANES
    cell_y = (cell_at // LANES) % height
    cell_z = cell_at // (LANES * height)
    plane_row = jnp.where(cell_z == 0, cell_y, height + cell_z)
    x_map = jnp.where(iota((LANES, LANES), 0) == cell_x, 1.0, 0.0)
    plane_rows = height + depth
    plane_map = jnp.where(iota((plane_rows, LANES), 0) == plane_row, 1.0, 0.0)

    loads[4].wait()
    owned_rows = front.shape[1]
    chunk = 1024

    def split_front(i, carry):
        columns = pl.ds(pl.multiple_of(i * chunk, chunk), chunk)
        for k in range(2):
            value = front[k, :, columns]
            high = value.astype(BF16)
            split[k * owned_rows : (k + 1) * owned_rows, columns] = high
            split[(2 + k) * owned_rows : (3 + k) * owned_rows, columns] = (value - high.astype(F32)).astype(BF16)
        return carry

    lax.fori_loop(0, front.shape[2] // chunk, split_front, 0)

    loads[1].wait()
    for copy in x_halo:
        copy.wait()

    def residual_of(r, carry):
        re, im = operator(x, 0, r)
        re = rhs[0, r] - re
        im = rhs[1, r] - im
        res[0, r] = re
        res[1, r] = im
        drn[0, r] = re * coef[0] + im * coef[1]
        drn[1, r] = im * coef[0] - re * coef[1]
        return carry

    lax.fori_loop(0, rhs_count, residual_of, 0)

    planes = jnp.concatenate(
        [
            res[:, :, 0].reshape(comps, height, LANES),
            res[:, :, :, 0, :].reshape(comps, depth, LANES),
        ],
        axis=1,
    ).reshape(comps * plane_rows, LANES)
    hits = dot(planes, x_map, (1, 0)).reshape(comps, plane_rows, LANES)
    values = jnp.sum(hits * plane_map[None], axis=1)
    values = jnp.concatenate([values, jnp.zeros((LANES - comps, LANES), F32)], axis=0)
    slot_send[:, 0, :] = pack_slots(values.T, tiles)
    send_rows(slot_send, slot_got, 0)
    slot_got[pl.ds(t, 1)] = slot_send[pl.ds(t, 1)]
    wait_rows(slot_send, slot_got, 0)

    by_slot = unpack_slots(slot_got[:, 0, :])
    lane = iota((8, LANES), 1)
    rows4 = jnp.concatenate([row_map[:, : 3 * tiles]] * (LANES // owned_rows), axis=0)
    wide = lax.dot_general(
        by_slot, rows4, (((0,), (1,)), ((), ())), precision=HIGHEST, preferred_element_type=F32
    )
    first, second = wide[:8], wide[8:16]
    block = jnp.where(
        lane < 32, first,
        jnp.where(lane < 64, pltpu.roll(first, 4, 0), jnp.where(lane < 96, second, pltpu.roll(second, 4, 0))),
    )
    own_send[...] = block[:4]
    spread(own_send, own_got, 1)
    own_got[t] = block[:4]
    wait_spread(own_send, own_got, 1)

    groups = tiles // 4
    got = own_got[...].reshape(groups, 4, 4, LANES)
    lane3 = iota((groups, 4, LANES), 2)
    for m in range(4):
        mine = None
        for b in range(4):
            shift = ((b - m) * 32) % LANES
            piece = got[:, b] if shift == 0 else pltpu.roll(got[:, b], shift, 2)
            mine = piece if mine is None else jnp.where(lane3 < 32 * b, mine, piece)
        vectors[pl.ds(g * groups, groups), 4 * m : 4 * m + 4, :] = mine

    def slab_copy(j, src_slab, peer):
        where = pl.ds(src_slab * groups, groups)
        return remote(
            vectors.at[where], vectors.at[where], slab_send_sem.at[0, j], slab_recv_sem.at[0, j], peer, t
        )

    for j in range(1, slabs):
        slab_copy(j, g, lax.rem(g + j, slabs)).start()

    total = jnp.zeros((4 * owned_rows, LANES), F32)
    for j in range(slabs):
        source = lax.rem(g + slabs - j, slabs)
        if j > 0:
            slab_copy(j, source, source).wait_recv()
        vec = jnp.concatenate([vectors[source * groups + a] for a in range(groups)], axis=1)
        high = vec.astype(BF16)
        low = (vec - high.astype(F32)).astype(BF16)
        both = jnp.concatenate([high, low, jnp.zeros((LANES - 2 * comps, vec.shape[1]), BF16)], axis=0)
        width = groups * LANES
        columns = pl.ds(pl.multiple_of(source * width, width), width)
        total = total + lax.dot_general(
            split[:, columns], both, (((1,), (1,)), ((), ())), preferred_element_type=F32
        )
    for j in range(1, slabs):
        slab_copy(j, g, lax.rem(g + j, slabs)).wait_send()
    parts = total[: 2 * owned_rows] + pltpu.roll(total[: 2 * owned_rows], LANES - comps, 1) + total[2 * owned_rows :]
    by_re, by_im = parts[:owned_rows], parts[owned_rows:]
    lane_own = iota((owned_rows, LANES), 1)
    solved = by_re + jnp.where(
        lane_own < rhs_count, -pltpu.roll(by_im, LANES - rhs_count, 1), pltpu.roll(by_im, rhs_count, 1)
    )

    back = lax.dot_general(
        row_map, solved, (((0,), (0,)), ((), ())), precision=HIGHEST, preferred_element_type=F32
    )
    ret_send[:, 0, :] = pack_slots(back, tiles)
    send_rows(ret_send, ret_got, 2)
    ret_got[pl.ds(t, 1)] = ret_send[pl.ds(t, 1)]
    wait_rows(ret_send, ret_got, 2)
    back = unpack_slots(ret_got[:, 0, :])
    back = jnp.concatenate([back, jnp.zeros((LANES - 3 * tiles, LANES), F32)], axis=0)
    values = back.T[:comps]
    placed = (values[:, None, :] * plane_map[None]).reshape(comps * plane_rows, LANES)
    extra = dot(placed, x_map, (1, 1)).reshape(2, rhs_count, plane_rows, LANES)
    drn[:, :, 0] = drn[:, :, 0] + extra[:, :, :height]
    drn[:, :, :, 0, :] = drn[:, :, :, 0, :] + extra[:, :, height:]

    pack_halo(drn, 1)
    d_halo = halo_copies(drn, 1)
    for copy in d_halo:
        copy.start()
    for copy in d_halo:
        copy.wait()

    acc[...] = jnp.zeros_like(acc)

    def image_of(r, carry):
        re, im = operator(drn, 1, r)
        img[0, r] = re
        img[1, r] = im
        res_re, res_im = res[0, r], res[1, r]
        for i, value in enumerate(
            [re * res_re + im * res_im, re * res_im - im * res_re, re * re + im * im]
        ):
            acc[pl.ds(i * rhs_count + r, 1), :] = jnp.sum(jnp.sum(value, axis=0), axis=0, keepdims=True)
        return carry

    lax.fori_loop(0, rhs_count, image_of, 0)

    ones = jnp.ones((8, LANES), F32)
    sum_send[...] = dot(ones, acc[...], (1, 1))[:1]
    spread(sum_send, sum_got, 3)
    sum_got[t] = sum_send[...]
    wait_spread(sum_send, sum_got, 3)
    sum2_send[...] = jnp.sum(sum_got[...], axis=0)

    def sum_copy(j, row, peer):
        return remote(
            sum2_send, sum2_got.at[row], slab_send_sem.at[1, j], slab_recv_sem.at[1, j], peer, t
        )

    for j in range(1, slabs):
        sum_copy(j, g, lax.rem(g + j, slabs)).start()
    sum2_got[g] = sum2_send[...]
    for j in range(1, slabs):
        source = lax.rem(g + slabs - j, slabs)
        sum_copy(j, source, source).wait()
    totals = dot(sum2_got[:, 0, :], jnp.ones((slabs, LANES), F32), (0, 0))
    denom = totals[2 * rhs_count : 3 * rhs_count] + 1e-06
    alpha[0] = totals[:rhs_count] / denom
    alpha[1] = totals[rhs_count : 2 * rhs_count] / denom

    def update(r, carry):
        a_re = alpha[0, pl.ds(r, 1), :][None]
        a_im = alpha[1, pl.ds(r, 1), :][None]
        d_re, d_im = drn[0, r], drn[1, r]
        sol_ref[0, r] = x[0, r] + a_re * d_re - a_im * d_im
        sol_ref[1, r] = x[1, r] + a_re * d_im + a_im * d_re
        i_re, i_im = img[0, r], img[1, r]
        new_ref[0, r] = res[0, r] - a_re * i_re + a_im * i_im
        new_ref[1, r] = res[1, r] - a_re * i_im - a_im * i_re
        return carry

    lax.fori_loop(0, rhs_count, update, 0)


def local(x_start, rhs, wave_sq, damping, front, front_order, pair_count, sep_cell):
    slabs, tiles = lax.axis_size("gz"), lax.axis_size("xy")
    _, rhs_count, depth, height, width = x_start.shape
    field = pltpu.VMEM(x_start.shape, F32)
    any_space = pl.BlockSpec(memory_space=pl.ANY)
    vmem = pl.BlockSpec(memory_space=pltpu.VMEM)
    rows = pltpu.VMEM((tiles, 1, LANES), F32)
    dma = pltpu.SemaphoreType.DMA
    return pl.pallas_call(
        step,
        out_shape=(
            jax.ShapeDtypeStruct(x_start.shape, F32),
            jax.ShapeDtypeStruct(x_start.shape, F32),
        ),
        in_specs=[any_space] * 5 + [vmem] * 3,
        out_specs=(vmem, vmem),
        scratch_shapes=[
            field,
            field,
            pltpu.VMEM(wave_sq.shape, F32),
            pltpu.VMEM(wave_sq.shape, F32),
            pltpu.VMEM(front.shape, F32),
            pltpu.VMEM((4 * front.shape[1], front.shape[2]), BF16),
            field,
            field,
            field,
            pltpu.VMEM((2,) + wave_sq.shape, F32),
            pltpu.VMEM((2, 2, 2, rhs_count, depth, width), F32),
            pltpu.VMEM((2, 4, 2, rhs_count, width), F32),
            pltpu.VMEM((2, 2, 2, rhs_count, height, width), F32),
            pltpu.VMEM((2, 2, 2, rhs_count, depth, width), F32),
            pltpu.VMEM((2, 4, 2, rhs_count, width), F32),
            rows,
            rows,
            pltpu.VMEM((4, LANES), F32),
            pltpu.VMEM((tiles, 4, LANES), F32),
            pltpu.VMEM((slabs * tiles // 4, 2 * rhs_count, LANES), F32),
            rows,
            rows,
            pltpu.VMEM((LANES, LANES), F32),
            pltpu.VMEM((1, LANES), F32),
            rows,
            pltpu.VMEM((1, LANES), F32),
            pltpu.VMEM((slabs, 1, LANES), F32),
            pltpu.VMEM((2, rhs_count, LANES), F32),
            dma((5,)),
            dma((2, 8)),
            dma((2, 8)),
            dma((4, tiles)),
            dma((4, tiles)),
            dma((2, slabs)),
            dma((2, slabs)),
        ],
        compiler_params=pltpu.CompilerParams(
            collective_id=0, has_side_effects=True, vmem_limit_bytes=60 * 1024 * 1024
        ),
    )(x_start, rhs, wave_sq, damping, front, front_order, pair_count, sep_cell)


def solution(mesh):
    in_specs = (
        P(None, None, "gz", "xy", None),
        P(None, None, "gz", "xy", None),
        P("gz", "xy", None),
        P("gz", "xy", None),
        P(None, ("gz", "xy"), None),
        P("gz", "xy", None),
        P("gz", None, None),
        P("gz", "xy", None),
    )
    out_specs = (P(None, None, "gz", "xy", None), P(None, None, "gz", "xy", None))
    return jax.shard_map(local, mesh=mesh, in_specs=in_specs, out_specs=out_specs, check_vma=False)
```

time: 357 us -> 71.6 us (0.20)
  blocking collectives: 236 us -> 0 us
  Pallas kernels: 0 us -> 67.4 us
  other arithmetic: 35.8 us -> 0 us
  starting transfers between devices: 33.7 us -> 0 us
  local copies, waits for them, and re-layouts: 31.7 us -> 3.36 us
  waiting for transfers between devices: 11 us -> 0 us
  matrix products: 6.99 us -> 0 us
    all_gather x3 -> x0, blocking collectives: 159 us -> none  [the longest x1 81.8 us: local(): part_vals = lax.all_gather(owned, ('gz', 'xy'), axis=1, tiled=True)]
    psum x1 -> x0, blocking collectives: 77.1 us -> none  [local(): totals = lax.psum(jnp.stack([num_real, num_imag, den_part]), ('gz', 'xy'))]
    pallas_call x0 -> x1, Pallas kernels: none -> 67.4 us  [local(): pl.pallas_call(step, out_shape=(jax.ShapeDtypeStruct(x_start.shape, F32),...]
    ppermute x8 -> x0, starting transfers between devices: 33.7 us -> none  [the longest x4 26 us: extended(): lax.ppermute(lax.slice_in_dim(block, block.shape[dim] - width, None, axis...]
    div x4 -> x0, other arithmetic: 12.2 us -> none  [the longest x2 12 us: apply_operator(): (128.0 * centre - 14.0 * face_sum - 3.0 * edge_sum - corner_sum) / 30.0]
    ppermute x8 -> x0, waiting for transfers between devices: 11 us -> none  [the longest x4 10.9 us: extended(): lax.ppermute(lax.slice_in_dim(block, 0, width, axis=dim), axis, backward)]
    gather x5 -> x0, local copies, waits for them, and re-layouts: 8.9 us -> none  [the longest x1 4 us: local(): slot_vals = jnp.take(flat_residual, sep_cells, axis=1) * valid_send[None, :]]
    dot_general x7 -> x0, matrix products: 6.99 us -> none  [the longest x1 2.29 us: local(): product(front_real, vals_real)]
  transfers between devices with their start and end apart: 8 -> 0, of which waited for: 4 -> 0; matrix products, arithmetic and copies ran while one was open for 3% -> 0% of each run, Pallas kernels for 0% -> 0%
where the time goes in v1:
time: 71.6 us; the launch traced here: 71.4 us
  Pallas kernels  67.4 us (94%)
  local copies, waits for them, and re-layouts  3.36 us (5%)
    pallas_call x1, Pallas kernels, local(): pl.pallas_call(step, out_shape=(jax.ShapeDtypeStruct(x_start.shape, F32),...  67.4 us
    unnamed x4, local copies, waits for them, and re-layouts  3.36 us

profile of v1, /device:TPU:1, one launch (start us, length us, event | category | flops | bytes accessed | tf_op | source)
XLA Modules:
  0.0 71.4 jit_solution(7848163694628983219)
XLA Ops:
  0.6 67.4 %shard_map.95 = (f32[2,8,8,16,128]{4,3,2,1,0:T(8,128)}, f32[2,8,8,16,128]{4,3,2,1,0:T(8,128)}) custom-call(f32[2,8,8,16,128]{4,3,2,1,0:T(8,128)} %x_hbm.1, f32[2,8,8,16,128]{4,3,2,1,0:T(8,128)} %rhs_hbm.1, f32[8,16,128]{2,1,0:T(8,128)} %wave_hbm.1, f32[8,16,128]{2,1,0:T(8,128)} %damp_hbm.1, f32[2,32,8192]{2,1,0:T(8,128)} %front_hbm.1, ...), custom_call_target="tpu_custom_call" | custom-call | tf_op jit(solution)/shard_map/pallas_call | solution.py:452
  68.1 0.0 copy-start
  68.1 2.4 %copy.12 = f32[2,8,8,16,128]{4,3,2,1,0:T(8,128)} copy(f32[2,8,8,16,128]{4,3,2,1,0:T(8,128)} %get-tuple-element.4) | data formatting | bytes 2097152
  70.5 0.0 copy-done
  70.5 1.0 %copy.13 = f32[2,8,8,16,128]{4,3,2,1,0:T(8,128)} copy(f32[2,8,8,16,128]{4,3,2,1,0:T(8,128)S(1)} %copy-done) | data formatting | bytes 2097152
Async XLA Ops:
  68.1 2.4 %copy-start = (f32[2,8,8,16,128]{4,3,2,1,0:T(8,128)S(1)}, f32[2,8,8,16,128]{4,3,2,1,0:T(8,128)}, u32[]{:S(2)}) copy-start(f32[2,8,8,16,128]{4,3,2,1,0:T(8,128)} %get-tuple-element.5) | copy-start | bytes 3145732

commit v2 on v1

--- a/solution.py
+++ b/solution.py
@@ -74,9 +74,9 @@
 
 
 def step(
-    x_hbm, rhs_hbm, wave_hbm, damp_hbm, front_hbm, order_ref, count_ref, cell_ref,
+    x_hbm, rhs_hbm, wave_hbm, damp_hbm, front_hbm, order_hbm, count_hbm, cell_hbm,
     sol_ref, new_ref,
-    x, rhs, wave, damp, front, split, res, drn, img, coef,
+    x, rhs, wave, damp, front, order_ref, count_ref, cell_ref, split, res, drn, img, coef,
     y_send, e_send, z_got, y_got, e_got,
     slot_send, slot_got, own_send, own_got, vectors, ret_send, ret_got, acc, sum_send, sum_got, sum2_send, sum2_got, alpha,
     load_sem, halo_send_sem, halo_recv_sem, tile_send_sem, tile_recv_sem, slab_send_sem, slab_recv_sem,
@@ -91,12 +91,13 @@
     loads = [
         pltpu.make_async_copy(src, dst, load_sem.at[i])
         for i, (src, dst) in enumerate(
-            [(x_hbm, x), (rhs_hbm, rhs), (wave_hbm, wave), (damp_hbm, damp), (front_hbm, front)]
+            [
+                (x_hbm, x), (rhs_hbm, rhs), (wave_hbm, wave), (damp_hbm, damp), (front_hbm, front),
+                (order_hbm, order_ref), (count_hbm, count_ref), (cell_hbm, cell_ref),
+            ]
         )
     ]
-    for copy in loads:
-        copy.start()
-
+    loads[0].start()
     barrier = pltpu.get_barrier_semaphore()
 
     def greet(gz, xy):
@@ -115,6 +116,8 @@
     for gz in (up_g, down_g):
         for xy in (up_t, down_t):
             greet(gz, xy)
+    for copy in loads[1:]:
+        copy.start()
 
     def remote(src, dst, send_sem, recv_sem, gz, xy):
         return pltpu.make_async_remote_copy(
@@ -217,7 +220,7 @@
     pack_halo(x, 0)
     x_halo = halo_copies(x, 0)
     pl.semaphore_wait(barrier, tiles - 1 + slabs - 1 + 4)
-    for copy in x_halo:
+    for copy in x_halo[::-1]:
         copy.start()
 
     loads[2].wait()
@@ -231,6 +234,8 @@
     coef[0] = diag_re / modulus
     coef[1] = diag_im / modulus
 
+    for copy in loads[5:]:
+        copy.wait()
     counts = count_ref[0, pl.ds(t, 1), :].astype(F32)
     spread_lane = iota((tiles, LANES), 1)
     spread_row = iota((tiles, LANES), 0)
@@ -335,31 +340,49 @@
             mine = piece if mine is None else jnp.where(lane3 < 32 * b, mine, piece)
         vectors[pl.ds(g * groups, groups), 4 * m : 4 * m + 4, :] = mine
 
-    def slab_copy(j, src_slab, peer):
-        where = pl.ds(src_slab * groups, groups)
+    partner = g + 1 - 2 * lax.rem(g, 2)
+    chips = slabs // 2
+
+    def slab_copy(j, source, peer):
+        where = pl.ds(source * groups, groups)
         return remote(
             vectors.at[where], vectors.at[where], slab_send_sem.at[0, j], slab_recv_sem.at[0, j], peer, t
         )
 
-    for j in range(1, slabs):
-        slab_copy(j, g, lax.rem(g + j, slabs)).start()
-
-    total = jnp.zeros((4 * owned_rows, LANES), F32)
-    for j in range(slabs):
-        source = lax.rem(g + slabs - j, slabs)
-        if j > 0:
-            slab_copy(j, source, source).wait_recv()
+    def back_of(base, j):
+        return lax.rem(base + slabs - 2 * j, slabs)
+
+    width = groups * LANES
+
+    def product(source):
         vec = jnp.concatenate([vectors[source * groups + a] for a in range(groups)], axis=1)
         high = vec.astype(BF16)
         low = (vec - high.astype(F32)).astype(BF16)
         both = jnp.concatenate([high, low, jnp.zeros((LANES - 2 * comps, vec.shape[1]), BF16)], axis=0)
-        width = groups * LANES
         columns = pl.ds(pl.multiple_of(source * width, width), width)
-        total = total + lax.dot_general(
+        return lax.dot_general(
             split[:, columns], both, (((1,), (1,)), ((), ())), preferred_element_type=F32
         )
-    for j in range(1, slabs):
-        slab_copy(j, g, lax.rem(g + j, slabs)).wait_send()
+
+    ring = sorted(range(1, chips), key=lambda j: -min(j, chips - j))
+    sends = [slab_copy(j, g, lax.rem(g + 2 * j, slabs)) for j in ring] + [slab_copy(chips, g, partner)]
+    for copy in sends:
+        copy.start()
+    total = product(g)
+    for j in ring[::-1]:
+        slab_copy(j, back_of(g, j), back_of(g, j)).wait_recv()
+        onward = slab_copy(chips + j, back_of(g, j), partner)
+        onward.start()
+        sends.append(onward)
+    slab_copy(chips, partner, partner).wait_recv()
+    total = total + product(partner)
+    for j in ring[::-1]:
+        total = total + product(back_of(g, j))
+    for j in ring[::-1]:
+        slab_copy(chips + j, back_of(partner, j), partner).wait_recv()
+        total = total + product(back_of(partner, j))
+    for copy in sends:
+        copy.wait_send()
     parts = total[: 2 * owned_rows] + pltpu.roll(total[: 2 * owned_rows], LANES - comps, 1) + total[2 * owned_rows :]
     by_re, by_im = parts[:owned_rows], parts[owned_rows:]
     lane_own = iota((owned_rows, LANES), 1)
@@ -384,7 +407,7 @@
 
     pack_halo(drn, 1)
     d_halo = halo_copies(drn, 1)
-    for copy in d_halo:
+    for copy in d_halo[::-1]:
         copy.start()
     for copy in d_halo:
         copy.wait()
@@ -451,11 +474,8 @@
     dma = pltpu.SemaphoreType.DMA
     return pl.pallas_call(
         step,
-        out_shape=(
-            jax.ShapeDtypeStruct(x_start.shape, F32),
-            jax.ShapeDtypeStruct(x_start.shape, F32),
-        ),
-        in_specs=[any_space] * 5 + [vmem] * 3,
+        out_shape=(field, field),
+        in_specs=[any_space] * 8,
         out_specs=(vmem, vmem),
         scratch_shapes=[
             field,
@@ -463,6 +483,9 @@
             pltpu.VMEM(wave_sq.shape, F32),
             pltpu.VMEM(wave_sq.shape, F32),
             pltpu.VMEM(front.shape, F32),
+            pltpu.VMEM(front_order.shape, jnp.int32),
+            pltpu.VMEM(pair_count.shape, jnp.int32),
+            pltpu.VMEM(sep_cell.shape, jnp.int32),
             pltpu.VMEM((4 * front.shape[1], front.shape[2]), BF16),
             field,
             field,
@@ -486,7 +509,7 @@
             pltpu.VMEM((1, LANES), F32),
             pltpu.VMEM((slabs, 1, LANES), F32),
             pltpu.VMEM((2, rhs_count, LANES), F32),
-            dma((5,)),
+            dma((8,)),
             dma((2, 8)),
             dma((2, 8)),
             dma((4, tiles)),

time: 71.6 us -> 67.6 us (0.944)
  Pallas kernels: 67.4 us -> 64.9 us
  local copies, waits for them, and re-layouts: 3.36 us -> 1.94 us
    pallas_call x1, Pallas kernels: 67.4 us -> 64.9 us  [local(): pl.pallas_call(step, out_shape=(field, field), in_specs=[any_space] * 8,...]
    unnamed x4 -> x2, local copies, waits for them, and re-layouts: 3.36 us -> 1.94 us
where the time goes in v2:
time: 67.6 us; the launch traced here: 67.5 us
  Pallas kernels  64.9 us (96%)
  local copies, waits for them, and re-layouts  1.94 us (3%)
    pallas_call x1, Pallas kernels, local(): pl.pallas_call(step, out_shape=(field, field), in_specs=[any_space] * 8,...  64.9 us
    unnamed x2, local copies, waits for them, and re-layouts  1.94 us

profile of v2, /device:TPU:1, one launch (start us, length us, event | category | flops | bytes accessed | tf_op | source)
XLA Modules:
  0.0 67.5 jit_solution(17894878466041582482)
XLA Ops:
  0.6 64.9 %shard_map.95 = (f32[2,8,8,16,128]{4,3,2,1,0:T(8,128)S(1)}, f32[2,8,8,16,128]{4,3,2,1,0:T(8,128)S(1)}) custom-call(f32[2,8,8,16,128]{4,3,2,1,0:T(8,128)} %x_hbm.1, f32[2,8,8,16,128]{4,3,2,1,0:T(8,128)} %rhs_hbm.1, f32[8,16,128]{2,1,0:T(8,128)} %wave_hbm.1, f32[8,16,128]{2,1,0:T(8,128)} %damp_hbm.1, f32[2,32,8192]{2,1,0:T(8,128)} %front_hbm.1, ...), custom_call_target="tpu_custom_call" | custom-call | tf_op jit(solution)/shard_map/pallas_call | solution.py:475
  65.5 1.0 %copy.12 = f32[2,8,8,16,128]{4,3,2,1,0:T(8,128)} copy(f32[2,8,8,16,128]{4,3,2,1,0:T(8,128)S(1)} %get-tuple-element.2) | data formatting | bytes 2097152
  66.5 1.0 %copy.13 = f32[2,8,8,16,128]{4,3,2,1,0:T(8,128)} copy(f32[2,8,8,16,128]{4,3,2,1,0:T(8,128)S(1)} %get-tuple-element.3) | data formatting | bytes 2097152

commit v3 on v2

--- a/solution.py
+++ b/solution.py
@@ -22,6 +22,21 @@
     return lax.dot_general(
         a, b, ((contract[:1], contract[1:]), ((), ())), precision=HIGHEST, preferred_element_type=F32
     )
+
+
+def in_parts(value):
+    high = value.astype(BF16)
+    rest = value - high.astype(F32)
+    middle = rest.astype(BF16)
+    return high, middle, (rest - middle.astype(F32)).astype(BF16)
+
+
+def pick_rows(value, one_hot, contract):
+    rows = value.shape[0]
+    out = lax.dot_general(
+        jnp.concatenate(in_parts(value), axis=0), one_hot, (((1,), (contract,)), ((), ())), preferred_element_type=F32
+    )
+    return out[:rows] + out[rows : 2 * rows] + out[2 * rows :]
 
 
 def x_sum(u):
@@ -78,8 +93,8 @@
     sol_ref, new_ref,
     x, rhs, wave, damp, front, order_ref, count_ref, cell_ref, split, res, drn, img, coef,
     y_send, e_send, z_got, y_got, e_got,
-    slot_send, slot_got, own_send, own_got, vectors, ret_send, ret_got, acc, sum_send, sum_got, sum2_send, sum2_got, alpha,
-    load_sem, halo_send_sem, halo_recv_sem, tile_send_sem, tile_recv_sem, slab_send_sem, slab_recv_sem,
+    slot_send, slot_got, own_send, own_got, vectors, ret_send, ret_got, fix_send, fix_got, cells_got, x_maps, acc, sum_send, sum_got, sum2_send, sum2_got, alpha,
+    load_sem, cell_send_sem, cell_recv_sem, fix_send_sem, fix_recv_sem, halo_send_sem, halo_recv_sem, tile_send_sem, tile_recv_sem, slab_send_sem, slab_recv_sem,
 ):
     slabs, tiles = lax.axis_size("gz"), lax.axis_size("xy")
     g, t = lax.axis_index("gz"), lax.axis_index("xy")
@@ -219,8 +234,21 @@
     loads[0].wait()
     pack_halo(x, 0)
     x_halo = halo_copies(x, 0)
+    around = [(dg, dt) for dg in (-1, 0, 1) for dt in (-1, 0, 1)]
+    own = around.index((0, 0))
+    cell_copies = [
+        remote(
+            cell_ref.at[0], cells_got.at[n], cell_send_sem.at[n], cell_recv_sem.at[n],
+            lax.rem(g - dg + slabs, slabs), lax.rem(t - dt + tiles, tiles),
+        )
+        for n, (dg, dt) in enumerate(around)
+        if n not in (0, own)
+    ]
+    loads[7].wait()
+    for n in (0, own):
+        cells_got[n] = cell_ref[0]
     pl.semaphore_wait(barrier, tiles - 1 + slabs - 1 + 4)
-    for copy in x_halo[::-1]:
+    for copy in x_halo[::-1] + cell_copies:
         copy.start()
 
     loads[2].wait()
@@ -234,7 +262,7 @@
     coef[0] = diag_re / modulus
     coef[1] = diag_im / modulus
 
-    for copy in loads[5:]:
+    for copy in loads[5:7]:
         copy.wait()
     counts = count_ref[0, pl.ds(t, 1), :].astype(F32)
     spread_lane = iota((tiles, LANES), 1)
@@ -251,20 +279,24 @@
     order_map = jnp.where(iota((tiles, tiles), 0) == order, 1.0, 0.0)
     row_map = dot(order_map, entry_map, (1, 0))
 
-    cells = jnp.broadcast_to(cell_ref[0, 0:1, :].astype(F32), (8, cell_ref.shape[2]))
     slots = cell_ref.shape[2]
     slot_row = iota((slots, LANES), 0)
     slot_lane = iota((slots, LANES), 1)
     slot_pick = jnp.where(
         (slot_lane < slots) & (slot_row == 3 * (slot_lane % tiles) + slot_lane // tiles), 1.0, 0.0
     )
-    cell_at = (dot(cells, slot_pick, (1, 0))[:1] + 0.5).astype(jnp.int32)
-    cell_x = cell_at % LANES
-    cell_y = (cell_at // LANES) % height
-    cell_z = cell_at // (LANES * height)
+    plane_rows = height + depth
+
+    def places(cells):
+        cell_at = (dot(cells.astype(F32), slot_pick, (1, 0)) + 0.5).astype(jnp.int32)
+        return cell_at % LANES, (cell_at // LANES) % height, cell_at // (LANES * height)
+
+    def x_map_of(cell_x):
+        return jnp.where(iota((LANES, LANES), 0) == cell_x, 1.0, 0.0).astype(BF16)
+
+    cell_x, cell_y, cell_z = [v[:1] for v in places(jnp.broadcast_to(cell_ref[0], (8, slots)))]
+    x_map = x_map_of(cell_x)
     plane_row = jnp.where(cell_z == 0, cell_y, height + cell_z)
-    x_map = jnp.where(iota((LANES, LANES), 0) == cell_x, 1.0, 0.0)
-    plane_rows = height + depth
     plane_map = jnp.where(iota((plane_rows, LANES), 0) == plane_row, 1.0, 0.0)
 
     loads[4].wait()
@@ -305,20 +337,29 @@
         ],
         axis=1,
     ).reshape(comps * plane_rows, LANES)
-    hits = dot(planes, x_map, (1, 0)).reshape(comps, plane_rows, LANES)
+    hits = pick_rows(planes, x_map, 0).reshape(comps, plane_rows, LANES)
     values = jnp.sum(hits * plane_map[None], axis=1)
     values = jnp.concatenate([values, jnp.zeros((LANES - comps, LANES), F32)], axis=0)
     slot_send[:, 0, :] = pack_slots(values.T, tiles)
     send_rows(slot_send, slot_got, 0)
     slot_got[pl.ds(t, 1)] = slot_send[pl.ds(t, 1)]
+
+    pack_halo(drn, 1)
+    d_halo = halo_copies(drn, 1)
+    for copy in d_halo[::-1]:
+        copy.start()
+    for copy in cell_copies:
+        copy.wait()
+    near_x, near_y, near_z = places(cells_got[:, 0, :])
+    for n in range(len(around)):
+        x_maps[n] = x_map_of(near_x[n : n + 1])
+
     wait_rows(slot_send, slot_got, 0)
 
     by_slot = unpack_slots(slot_got[:, 0, :])
     lane = iota((8, LANES), 1)
     rows4 = jnp.concatenate([row_map[:, : 3 * tiles]] * (LANES // owned_rows), axis=0)
-    wide = lax.dot_general(
-        by_slot, rows4, (((0,), (1,)), ((), ())), precision=HIGHEST, preferred_element_type=F32
-    )
+    wide = pick_rows(by_slot.T[:comps], rows4.astype(BF16), 1)
     first, second = wide[:8], wide[8:16]
     block = jnp.where(
         lane < 32, first,
@@ -391,26 +432,71 @@
     )
 
     back = lax.dot_general(
-        row_map, solved, (((0,), (0,)), ((), ())), precision=HIGHEST, preferred_element_type=F32
+        row_map.astype(BF16), jnp.concatenate(in_parts(solved), axis=1), (((0,), (0,)), ((), ())),
+        preferred_element_type=F32,
     )
-    ret_send[:, 0, :] = pack_slots(back, tiles)
-    send_rows(ret_send, ret_got, 2)
-    ret_got[pl.ds(t, 1)] = ret_send[pl.ds(t, 1)]
-    wait_rows(ret_send, ret_got, 2)
-    back = unpack_slots(ret_got[:, 0, :])
-    back = jnp.concatenate([back, jnp.zeros((LANES - 3 * tiles, LANES), F32)], axis=0)
-    values = back.T[:comps]
-    placed = (values[:, None, :] * plane_map[None]).reshape(comps * plane_rows, LANES)
-    extra = dot(placed, x_map, (1, 1)).reshape(2, rhs_count, plane_rows, LANES)
+    packed = pack_slots(back[:, :LANES] + back[:, LANES : 2 * LANES] + back[:, 2 * LANES :], tiles)
+    ret_send[1 : tiles + 1, 0, :] = packed
+    ret_send[0] = packed[tiles - 1 :]
+    ret_send[tiles + 1] = packed[:1]
+
+    def ret_copy(peer, row):
+        return remote(
+            ret_send.at[pl.ds(peer, 3)], ret_got.at[row], tile_send_sem.at[2, peer], tile_recv_sem.at[2, row], g, peer
+        )
+
+    def start_ret(j, carry):
+        ret_copy(lax.rem(t + j, tiles), t).start()
+        return carry
+
+    def wait_ret(j, carry):
+        peer = lax.rem(t + j, tiles)
+        ret_copy(peer, peer).wait()
+        return carry
+
+    lax.fori_loop(1, tiles, start_ret, 0)
+    ret_got[t] = ret_send[pl.ds(t, 3)]
+    for copy in d_halo:
+        copy.wait()
+    lax.fori_loop(1, tiles, wait_ret, 0)
+    for i in range(3):
+        back = unpack_slots(ret_got[:, i, 0, :])
+        back = jnp.concatenate([back, jnp.zeros((LANES - 3 * tiles, LANES), F32)], axis=0)
+        fix_send[i] = back.T[:comps]
+    fix_copies = [
+        remote(fix_send, fix_got.at[i], fix_send_sem.at[i], fix_recv_sem.at[i], gz, t)
+        for i, gz in enumerate((up_g, down_g))
+    ]
+    for copy in fix_copies:
+        copy.start()
+
+    def place_rows(values, n, mask):
+        rows = mask.shape[0]
+        placed = (values[:, None, :] * mask[None]).reshape(comps * rows, LANES)
+        return pick_rows(placed, x_maps[n], 1).reshape(2, rhs_count, rows, LANES)
+
+    def place_row(values, n, z, y):
+        mask = jnp.where((near_z[n : n + 1] == z) & (near_y[n : n + 1] == y), 1.0, 0.0)
+        return pick_rows(values * mask, x_maps[n], 1).reshape(2, rhs_count, LANES)
+
+    extra = place_rows(fix_send[1], own, plane_map)
     drn[:, :, 0] = drn[:, :, 0] + extra[:, :, :height]
     drn[:, :, :, 0, :] = drn[:, :, :, 0, :] + extra[:, :, height:]
-
-    pack_halo(drn, 1)
-    d_halo = halo_copies(drn, 1)
-    for copy in d_halo[::-1]:
-        copy.start()
-    for copy in d_halo:
+    n = around.index((0, 1))
+    face = jnp.where((near_y[n : n + 1] == 0) & (iota((depth, LANES), 0) == near_z[n : n + 1]), 1.0, 0.0)
+    y_got[1, 1] = y_got[1, 1] + place_rows(fix_send[2], n, face)
+    n = around.index((0, -1))
+    y_got[1, 0, :, :, 0, :] = y_got[1, 0, :, :, 0, :] + place_row(fix_send[0], n, 0, height - 1)
+    for copy in fix_copies:
         copy.wait()
+    n = around.index((1, 0))
+    face = jnp.where((near_z[n : n + 1] == 0) & (iota((height, LANES), 0) == near_y[n : n + 1]), 1.0, 0.0)
+    z_got[1, 1] = z_got[1, 1] + place_rows(fix_got[1, 1], n, face)
+    n = around.index((-1, 0))
+    z_got[1, 0, :, :, 0, :] = z_got[1, 0, :, :, 0, :] + place_row(fix_got[0, 1], n, depth - 1, 0)
+    e_got[1, 3] = e_got[1, 3] + place_row(fix_got[1, 2], around.index((1, 1)), 0, 0)
+    e_got[1, 2] = e_got[1, 2] + place_row(fix_got[1, 0], around.index((1, -1)), 0, height - 1)
+    e_got[1, 1] = e_got[1, 1] + place_row(fix_got[0, 2], around.index((-1, 1)), depth - 1, 0)
 
     acc[...] = jnp.zeros_like(acc)
 
@@ -501,8 +587,12 @@
             pltpu.VMEM((4, LANES), F32),
             pltpu.VMEM((tiles, 4, LANES), F32),
             pltpu.VMEM((slabs * tiles // 4, 2 * rhs_count, LANES), F32),
-            rows,
-            rows,
+            pltpu.VMEM((tiles + 2, 1, LANES), F32),
+            pltpu.VMEM((tiles, 3, 1, LANES), F32),
+            pltpu.VMEM((3, 2 * rhs_count, LANES), F32),
+            pltpu.VMEM((2, 3, 2 * rhs_count, LANES), F32),
+            pltpu.VMEM((9, 1, sep_cell.shape[2]), jnp.int32),
+            pltpu.VMEM((9, LANES, LANES), BF16),
             pltpu.VMEM((LANES, LANES), F32),
             pltpu.VMEM((1, LANES), F32),
             rows,
@@ -510,6 +600,10 @@
             pltpu.VMEM((slabs, 1, LANES), F32),
             pltpu.VMEM((2, rhs_count, LANES), F32),
             dma((8,)),
+            dma((9,)),
+            dma((9,)),
+            dma((2,)),
+            dma((2,)),
             dma((2, 8)),
             dma((2, 8)),
             dma((4, tiles)),

time: 67.6 us -> 64.1 us (0.948)
  Pallas kernels: 64.9 us -> 61.5 us
    pallas_call x1, Pallas kernels: 64.9 us -> 61.5 us  [local(): pl.pallas_call(step, out_shape=(field, field), in_specs=[any_space] * 8,...]
where the time goes in v3:
time: 64.1 us; the launch traced here: 64 us
  Pallas kernels  61.5 us (96%)
  local copies, waits for them, and re-layouts  1.94 us (3%)
    pallas_call x1, Pallas kernels, local(): pl.pallas_call(step, out_shape=(field, field), in_specs=[any_space] * 8,...  61.5 us
    unnamed x2, local copies, waits for them, and re-layouts  1.94 us

profile of v3, /device:TPU:1, one launch (start us, length us, event | category | flops | bytes accessed | tf_op | source)
XLA Modules:
  0.0 64.0 jit_solution(7215872058125140344)
XLA Ops:
  0.6 61.5 %shard_map.95 = (f32[2,8,8,16,128]{4,3,2,1,0:T(8,128)S(1)}, f32[2,8,8,16,128]{4,3,2,1,0:T(8,128)S(1)}) custom-call(f32[2,8,8,16,128]{4,3,2,1,0:T(8,128)} %x_hbm.1, f32[2,8,8,16,128]{4,3,2,1,0:T(8,128)} %rhs_hbm.1, f32[8,16,128]{2,1,0:T(8,128)} %wave_hbm.1, f32[8,16,128]{2,1,0:T(8,128)} %damp_hbm.1, f32[2,32,8192]{2,1,0:T(8,128)} %front_hbm.1, ...), custom_call_target="tpu_custom_call" | custom-call | tf_op jit(solution)/shard_map/pallas_call | solution.py:561
  62.1 1.0 %copy.12 = f32[2,8,8,16,128]{4,3,2,1,0:T(8,128)} copy(f32[2,8,8,16,128]{4,3,2,1,0:T(8,128)S(1)} %get-tuple-element.2) | data formatting | bytes 2097152
  63.1 1.0 %copy.13 = f32[2,8,8,16,128]{4,3,2,1,0:T(8,128)} copy(f32[2,8,8,16,128]{4,3,2,1,0:T(8,128)S(1)} %get-tuple-element.3) | data formatting | bytes 2097152

commit v4 on v3

--- a/solution.py
+++ b/solution.py
@@ -58,6 +58,38 @@
     below = jnp.where(z_pos == 0, m2_edge, pltpu.roll(m2, 1, 0))
     above = jnp.where(z_pos == depth - 1, m2_edge, pltpu.roll(m2, depth - 1, 0))
     return m1 + below + above
+
+
+def plane_term(plane, edge_low=None, edge_high=None):
+    height = plane.shape[0]
+    p = x_sum(plane)
+    m2 = 3.0 * plane + p
+    y_pos = iota(plane.shape, 0)
+    m2_edge = 0.0
+    if edge_low is not None:
+        edge = jnp.where(y_pos == 0, edge_low, edge_high)
+        m2_edge = 3.0 * edge + x_sum(edge)
+    before = jnp.where(y_pos == 0, m2_edge, pltpu.roll(m2, 1, 0))
+    after = jnp.where(y_pos == height - 1, m2_edge, pltpu.roll(m2, height - 1, 0))
+    return 14.0 * plane + 3.0 * p + before + after
+
+
+def laplace_inside(centre):
+    depth, height, _ = centre.shape
+    blank = jnp.zeros_like(centre[:1])
+
+    def z_sum(u):
+        return jnp.concatenate([blank, u[:-1]], axis=0) + jnp.concatenate([u[1:], blank], axis=0)
+
+    p = x_sum(centre)
+    m1 = 14.0 * centre + 3.0 * p
+    m2 = 3.0 * centre + p
+    same = 128.0 * centre - 14.0 * p - z_sum(m1)
+    side = m1 + z_sum(m2)
+    y_pos = iota(centre.shape, 1)
+    before = jnp.where(y_pos == 0, 0.0, pltpu.roll(side, 1, 1))
+    after = jnp.where(y_pos == height - 1, 0.0, pltpu.roll(side, height - 1, 1))
+    return (same - before - after) * (1.0 / 30.0)
 
 
 def laplace(centre, z_low, z_high, y_low, y_high, edges):
@@ -90,10 +122,10 @@
 
 def step(
     x_hbm, rhs_hbm, wave_hbm, damp_hbm, front_hbm, order_hbm, count_hbm, cell_hbm,
-    sol_ref, new_ref,
-    x, rhs, wave, damp, front, order_ref, count_ref, cell_ref, split, res, drn, img, coef,
+    x, drn, res, img, alpha,
+    rhs, wave, damp, front, order_ref, count_ref, cell_ref, split, coef,
     y_send, e_send, z_got, y_got, e_got,
-    slot_send, slot_got, own_send, own_got, vectors, ret_send, ret_got, fix_send, fix_got, cells_got, x_maps, acc, sum_send, sum_got, sum2_send, sum2_got, alpha,
+    slot_send, slot_got, own_send, own_got, vectors, ret_send, ret_got, fix_send, fix_got, cells_got, x_maps, z_fix, e_fix, acc, sum_send, sum_got, sum2_send, sum2_got,
     load_sem, cell_send_sem, cell_recv_sem, fix_send_sem, fix_recv_sem, halo_send_sem, halo_recv_sem, tile_send_sem, tile_recv_sem, slab_send_sem, slab_recv_sem,
 ):
     slabs, tiles = lax.axis_size("gz"), lax.axis_size("xy")
@@ -170,25 +202,18 @@
     has_down_t = (t > 0).astype(F32)
     has_up_t = (t < tiles - 1).astype(F32)
 
-    def operator(field, which, r):
-        parts = []
-        for k in range(2):
-            edges = [
-                e_got[which, i, k, pl.ds(r, 1), :] * flag
-                for i, flag in enumerate(
-                    [has_down_g * has_down_t, has_down_g * has_up_t, has_up_g * has_down_t, has_up_g * has_up_t]
-                )
-            ]
-            parts.append(
-                laplace(
-                    field[k, r],
-                    z_got[which, 0, k, r] * has_down_g,
-                    z_got[which, 1, k, r] * has_up_g,
-                    y_got[which, 0, k, r] * has_down_t,
-                    y_got[which, 1, k, r] * has_up_t,
-                    edges,
-                )
-            )
+    def halo_of(which, k, r):
+        flags = [has_down_g * has_down_t, has_down_g * has_up_t, has_up_g * has_down_t, has_up_g * has_up_t]
+        edges = [e_got[which, i, k, pl.ds(r, 1), :] * flag for i, flag in enumerate(flags)]
+        return (
+            z_got[which, 0, k, r] * has_down_g,
+            z_got[which, 1, k, r] * has_up_g,
+            y_got[which, 0, k, r] * has_down_t,
+            y_got[which, 1, k, r] * has_up_t,
+            edges,
+        )
+
+    def diagonal(field, r, parts):
         re, im = field[0, r], field[1, r]
         w, wd = wave[...], damp[...]
         return parts[0] - w * re + wd * im, parts[1] - w * im - wd * re
@@ -299,36 +324,30 @@
     plane_row = jnp.where(cell_z == 0, cell_y, height + cell_z)
     plane_map = jnp.where(iota((plane_rows, LANES), 0) == plane_row, 1.0, 0.0)
 
-    loads[4].wait()
-    owned_rows = front.shape[1]
-    chunk = 1024
-
-    def split_front(i, carry):
-        columns = pl.ds(pl.multiple_of(i * chunk, chunk), chunk)
-        for k in range(2):
-            value = front[k, :, columns]
-            high = value.astype(BF16)
-            split[k * owned_rows : (k + 1) * owned_rows, columns] = high
-            split[(2 + k) * owned_rows : (3 + k) * owned_rows, columns] = (value - high.astype(F32)).astype(BF16)
-        return carry
-
-    lax.fori_loop(0, front.shape[2] // chunk, split_front, 0)
-
     loads[1].wait()
+
+    def residual_inside(r, carry):
+        re, im = diagonal(x, r, [laplace_inside(x[k, r]) for k in range(2)])
+        res[0, r] = rhs[0, r] - re
+        res[1, r] = rhs[1, r] - im
+        return carry
+
+    lax.fori_loop(0, rhs_count, residual_inside, 0)
     for copy in x_halo:
         copy.wait()
 
-    def residual_of(r, carry):
-        re, im = operator(x, 0, r)
-        re = rhs[0, r] - re
-        im = rhs[1, r] - im
-        res[0, r] = re
-        res[1, r] = im
-        drn[0, r] = re * coef[0] + im * coef[1]
-        drn[1, r] = im * coef[0] - re * coef[1]
-        return carry
-
-    lax.fori_loop(0, rhs_count, residual_of, 0)
+    def residual_edge(r, carry):
+        for k in range(2):
+            z_low, z_high, y_low, y_high, edges = halo_of(0, k, r)
+            res[k, r, 0] = res[k, r, 0] + plane_term(z_low) * (1.0 / 30.0)
+            res[k, r, depth - 1] = res[k, r, depth - 1] + plane_term(z_high) * (1.0 / 30.0)
+            low = side_rows(y_low, edges[0], edges[2]) * (1.0 / 30.0)
+            high = side_rows(y_high, edges[1], edges[3]) * (1.0 / 30.0)
+            res[k, r, :, 0, :] = res[k, r, :, 0, :] + low
+            res[k, r, :, height - 1, :] = res[k, r, :, height - 1, :] + high
+        return carry
+
+    lax.fori_loop(0, rhs_count, residual_edge, 0)
 
     planes = jnp.concatenate(
         [
@@ -344,6 +363,14 @@
     send_rows(slot_send, slot_got, 0)
     slot_got[pl.ds(t, 1)] = slot_send[pl.ds(t, 1)]
 
+    def scale(r, carry):
+        re, im = res[0, r], res[1, r]
+        drn[0, r] = re * coef[0] + im * coef[1]
+        drn[1, r] = im * coef[0] - re * coef[1]
+        return carry
+
+    lax.fori_loop(0, rhs_count, scale, 0)
+
     pack_halo(drn, 1)
     d_halo = halo_copies(drn, 1)
     for copy in d_halo[::-1]:
@@ -353,6 +380,21 @@
     near_x, near_y, near_z = places(cells_got[:, 0, :])
     for n in range(len(around)):
         x_maps[n] = x_map_of(near_x[n : n + 1])
+
+    loads[4].wait()
+    owned_rows = front.shape[1]
+    chunk = 1024
+
+    def split_front(i, carry):
+        columns = pl.ds(pl.multiple_of(i * chunk, chunk), chunk)
+        for k in range(2):
+            value = front[k, :, columns]
+            high = value.astype(BF16)
+            split[k * owned_rows : (k + 1) * owned_rows, columns] = high
+            split[(2 + k) * owned_rows : (3 + k) * owned_rows, columns] = (value - high.astype(F32)).astype(BF16)
+        return carry
+
+    lax.fori_loop(0, front.shape[2] // chunk, split_front, 0)
 
     wait_rows(slot_send, slot_got, 0)
 
@@ -487,31 +529,51 @@
     y_got[1, 1] = y_got[1, 1] + place_rows(fix_send[2], n, face)
     n = around.index((0, -1))
     y_got[1, 0, :, :, 0, :] = y_got[1, 0, :, :, 0, :] + place_row(fix_send[0], n, 0, height - 1)
+    acc[...] = jnp.zeros_like(acc)
+
+    def add_up(r, re, im, res_re, res_im):
+        for i, value in enumerate(
+            [re * res_re + im * res_im, re * res_im - im * res_re, re * re + im * im]
+        ):
+            row = pl.ds(i * rhs_count + r, 1)
+            acc[row, :] = acc[row, :] + jnp.sum(jnp.sum(value, axis=0), axis=0, keepdims=True)
+
+    def image_of(r, carry):
+        re, im = diagonal(drn, r, [laplace(drn[k, r], *halo_of(1, k, r)) for k in range(2)])
+        img[0, r] = re
+        img[1, r] = im
+        add_up(r, re[1:-1], im[1:-1], res[0, r, 1 : depth - 1], res[1, r, 1 : depth - 1])
+        return carry
+
+    lax.fori_loop(0, rhs_count, image_of, 0)
+
     for copy in fix_copies:
         copy.wait()
     n = around.index((1, 0))
     face = jnp.where((near_z[n : n + 1] == 0) & (iota((height, LANES), 0) == near_y[n : n + 1]), 1.0, 0.0)
-    z_got[1, 1] = z_got[1, 1] + place_rows(fix_got[1, 1], n, face)
-    n = around.index((-1, 0))
-    z_got[1, 0, :, :, 0, :] = z_got[1, 0, :, :, 0, :] + place_row(fix_got[0, 1], n, depth - 1, 0)
-    e_got[1, 3] = e_got[1, 3] + place_row(fix_got[1, 2], around.index((1, 1)), 0, 0)
-    e_got[1, 2] = e_got[1, 2] + place_row(fix_got[1, 0], around.index((1, -1)), 0, height - 1)
-    e_got[1, 1] = e_got[1, 1] + place_row(fix_got[0, 2], around.index((-1, 1)), depth - 1, 0)
-
-    acc[...] = jnp.zeros_like(acc)
-
-    def image_of(r, carry):
-        re, im = operator(drn, 1, r)
-        img[0, r] = re
-        img[1, r] = im
-        res_re, res_im = res[0, r], res[1, r]
-        for i, value in enumerate(
-            [re * res_re + im * res_im, re * res_im - im * res_re, re * re + im * im]
-        ):
-            acc[pl.ds(i * rhs_count + r, 1), :] = jnp.sum(jnp.sum(value, axis=0), axis=0, keepdims=True)
-        return carry
-
-    lax.fori_loop(0, rhs_count, image_of, 0)
+    z_fix[1] = place_rows(fix_got[1, 1], n, face) * has_up_g
+    z_fix[0] = jnp.zeros_like(z_fix[0])
+    z_fix[0, :, :, 0, :] = place_row(fix_got[0, 1], around.index((-1, 0)), depth - 1, 0) * has_down_g
+    e_fix[0] = place_row(fix_got[0, 2], around.index((-1, 1)), depth - 1, 0) * (has_down_g * has_up_t)
+    e_fix[1] = place_row(fix_got[1, 0], around.index((1, -1)), 0, height - 1) * (has_up_g * has_down_t)
+    e_fix[2] = place_row(fix_got[1, 2], around.index((1, 1)), 0, 0) * (has_up_g * has_up_t)
+
+    def image_edge(r, carry):
+        row = pl.ds(r, 1)
+        ends = [[], []]
+        for k in range(2):
+            low = plane_term(z_fix[0, k, r], jnp.zeros((1, LANES), F32), e_fix[0, k, row, :])
+            high = plane_term(z_fix[1, k, r], e_fix[1, k, row, :], e_fix[2, k, row, :])
+            for side, (z, term) in enumerate(((0, low), (depth - 1, high))):
+                value = img[k, r, z] - term * (1.0 / 30.0)
+                img[k, r, z] = value
+                ends[side].append(value)
+        both = [jnp.stack([ends[0][k], ends[1][k]]) for k in range(2)]
+        mine = [jnp.stack([res[k, r, 0], res[k, r, depth - 1]]) for k in range(2)]
+        add_up(r, both[0], both[1], mine[0], mine[1])
+        return carry
+
+    lax.fori_loop(0, rhs_count, image_edge, 0)
 
     ones = jnp.ones((8, LANES), F32)
     sum_send[...] = dot(ones, acc[...], (1, 1))[:1]
@@ -536,18 +598,17 @@
     alpha[0] = totals[:rhs_count] / denom
     alpha[1] = totals[rhs_count : 2 * rhs_count] / denom
 
-    def update(r, carry):
-        a_re = alpha[0, pl.ds(r, 1), :][None]
-        a_im = alpha[1, pl.ds(r, 1), :][None]
-        d_re, d_im = drn[0, r], drn[1, r]
-        sol_ref[0, r] = x[0, r] + a_re * d_re - a_im * d_im
-        sol_ref[1, r] = x[1, r] + a_re * d_im + a_im * d_re
-        i_re, i_im = img[0, r], img[1, r]
-        new_ref[0, r] = res[0, r] - a_re * i_re + a_im * i_im
-        new_ref[1, r] = res[1, r] - a_re * i_im - a_im * i_re
-        return carry
-
-    lax.fori_loop(0, rhs_count, update, 0)
+
+def update(x_ref, drn_ref, res_ref, img_ref, alpha_ref, sol_ref, new_ref):
+    r = pl.program_id(0)
+    a_re = alpha_ref[0, pl.ds(r, 1), :][None]
+    a_im = alpha_ref[1, pl.ds(r, 1), :][None]
+    d_re, d_im = drn_ref[0, r], drn_ref[1, r]
+    sol_ref[0, 0] = x_ref[0, r] + a_re * d_re - a_im * d_im
+    sol_ref[1, 0] = x_ref[1, r] + a_re * d_im + a_im * d_re
+    i_re, i_im = img_ref[0, r], img_ref[1, r]
+    new_ref[0, 0] = res_ref[0, r] - a_re * i_re + a_im * i_im
+    new_ref[1, 0] = res_ref[1, r] - a_re * i_im - a_im * i_re
 
 
 def local(x_start, rhs, wave_sq, damping, front, front_order, pair_count, sep_cell):
@@ -558,13 +619,12 @@
     vmem = pl.BlockSpec(memory_space=pltpu.VMEM)
     rows = pltpu.VMEM((tiles, 1, LANES), F32)
     dma = pltpu.SemaphoreType.DMA
-    return pl.pallas_call(
+    kept = pl.pallas_call(
         step,
-        out_shape=(field, field),
+        out_shape=(field, field, field, field, pltpu.VMEM((2, rhs_count, LANES), F32)),
         in_specs=[any_space] * 8,
-        out_specs=(vmem, vmem),
+        out_specs=(vmem,) * 5,
         scratch_shapes=[
-            field,
             field,
             pltpu.VMEM(wave_sq.shape, F32),
             pltpu.VMEM(wave_sq.shape, F32),
@@ -573,9 +633,6 @@
             pltpu.VMEM(pair_count.shape, jnp.int32),
             pltpu.VMEM(sep_cell.shape, jnp.int32),
             pltpu.VMEM((4 * front.shape[1], front.shape[2]), BF16),
-            field,
-            field,
-            field,
             pltpu.VMEM((2,) + wave_sq.shape, F32),
             pltpu.VMEM((2, 2, 2, rhs_count, depth, width), F32),
             pltpu.VMEM((2, 4, 2, rhs_count, width), F32),
@@ -593,12 +650,13 @@
             pltpu.VMEM((2, 3, 2 * rhs_count, LANES), F32),
             pltpu.VMEM((9, 1, sep_cell.shape[2]), jnp.int32),
             pltpu.VMEM((9, LANES, LANES), BF16),
+            pltpu.VMEM((2, 2, rhs_count, height, width), F32),
+            pltpu.VMEM((3, 2, rhs_count, width), F32),
             pltpu.VMEM((LANES, LANES), F32),
             pltpu.VMEM((1, LANES), F32),
             rows,
             pltpu.VMEM((1, LANES), F32),
             pltpu.VMEM((slabs, 1, LANES), F32),
-            pltpu.VMEM((2, rhs_count, LANES), F32),
             dma((8,)),
             dma((9,)),
             dma((9,)),
@@ -612,9 +670,21 @@
             dma((2, slabs)),
         ],
         compiler_params=pltpu.CompilerParams(
-            collective_id=0, has_side_effects=True, vmem_limit_bytes=60 * 1024 * 1024
+            collective_id=0, has_side_effects=True, vmem_limit_bytes=58600000
         ),
     )(x_start, rhs, wave_sq, damping, front, front_order, pair_count, sep_cell)
+    block = pl.BlockSpec((2, 1, depth, height, width), lambda r: (0, r, 0, 0, 0))
+    result = jax.ShapeDtypeStruct(x_start.shape, F32)
+    return tuple(
+        pl.pallas_call(
+            update,
+            grid=(rhs_count,),
+            out_shape=(result, result),
+            in_specs=[vmem] * 5,
+            out_specs=(block, block),
+            compiler_params=pltpu.CompilerParams(vmem_limit_bytes=16 * 1024 * 1024),
+        )(*kept)
+    )
 
 
 def solution(mesh):

time: 64.1 us -> 63.5 us (level)
  local copies, waits for them, and re-layouts: 1.94 us -> 0 us
  Pallas kernels: 61.5 us -> 62.7 us
    unnamed x2 -> x0, local copies, waits for them, and re-layouts: 1.94 us -> none
    pallas_call x1 -> x2, Pallas kernels: 61.5 us -> 62.7 us  [the longest x1 59.7 us: local(): pl.pallas_call(step, out_shape=(field, field, field, field, pltpu.VMEM((2...]
where the time goes in v4:
time: 63.5 us; the launch traced here: 63.4 us
  Pallas kernels  62.7 us (99%)
  between operations  0.64 us (1%)
    pallas_call x1, Pallas kernels, local(): pl.pallas_call(step, out_shape=(field, field, field, field, pltpu.VMEM((2...  59.7 us
    pallas_call x1, Pallas kernels, local(): pl.pallas_call(update, grid=(rhs_count,), out_shape=(result, result), in_...  3.05 us

profile of v4, /device:TPU:1, one launch (start us, length us, event | category | flops | bytes accessed | tf_op | source)
XLA Modules:
  0.0 63.4 jit_solution(2121308483952633131)
XLA Ops:
  0.6 59.7 %shard_map.95 = (f32[2,8,8,16,128]{4,3,2,1,0:T(8,128)S(1)}, f32[2,8,8,16,128]{4,3,2,1,0:T(8,128)S(1)}, f32[2,8,8,16,128]{4,3,2,1,0:T(8,128)S(1)}, f32[2,8,8,16,128]{4,3,2,1,0:T(8,128)S(1)}, f32[2,8,128]{2,1,0:T(8,128)S(1)}) custom-call(f32[2,8,8,16,128]{4,3,2,1,0:T(8,128)} %x_hbm.1, f32[2,8,8,16,128]{4,3,2,1,0:T(8,128)} %rhs_hbm.1, f32[8,16,128]{2,1,0:T(8,128)} %wave_hbm.1, ...), custom_call_target="tpu_custom_call" | custom-call | tf_op jit(solution)/shard_map/pallas_call | solution.py:622
  60.3 3.1 %shard_map.96 = (f32[2,8,8,16,128]{4,3,2,1,0:T(8,128)}, f32[2,8,8,16,128]{4,3,2,1,0:T(8,128)}) custom-call(f32[2,8,8,16,128]{4,3,2,1,0:T(8,128)S(1)} %get-tuple-element.7.x_ref, f32[2,8,8,16,128]{4,3,2,1,0:T(8,128)S(1)} %get-tuple-element.8.drn_ref, f32[2,8,8,16,128]{4,3,2,1,0:T(8,128)S(1)} %get-tuple-element.9.res_ref, ...), custom_call_target="tpu_custom_call" | custom-call | tf_op jit(solution)/shard_map/pallas_call | solution.py:679
